TPU v7x, 32 devices: a whole 2x2x4 slice. The times are simulated.
32 devices in a mesh: pair: 16 (over z, x, core), virt: 2 (over y).
Axes of the slice: x: 2, y: 2, z: 4, core: 2. Of those that a mesh axis runs over, the one named last changes fastest.
Arguments:
- amplitudes: bfloat16 [96, 96, 128, 128], P('pair', None, 'virt'), may hold values from -6 to 6
- integrals: bfloat16 [128, 20, 128, 128], P('virt'), may hold values from -0.125 to 0.125
- cd_tiles: int32 [128, 20], P('virt'), may hold values from 0 to 127, as said below
- tile_counts: int32 [128], P('virt'), may hold values from 10 to 20, as said below
- eps_occ: float32 [96], replicated, may hold values from -2 to -0.5
- eps_virt: float32 [128], replicated, may hold values from 0.5 to 3
Outputs:
- new_amplitudes: bfloat16 [96, 96, 128, 128], P('pair', None, 'virt')
Inputs may be any that keep to these rules, and one draw needn't show every extreme that they name: `cd_tiles`: row a holds 20 different numbers from lo(a) to lo(a) + 2 * 64 - 1, where lo(a) = min(max(a - 64, 0), 0); only its first tile_counts[a] entries are live. `tile_counts`: some entry equals 20.
All inputs are finite; a program needn't handle non-finite values.
Results may differ from a plain program's by a relative error of at most 0.001.
Values may be sent and summed in bfloat16 or wider, within the bound.
A program may use at most 448 MiB of HBM per device.

v0:
```python
import jax
import jax.numpy as jnp
from jax import lax
from jax.sharding import PartitionSpec as P


def extended(cells, sides, width):
    for axis, dim in sides:
        count = lax.axis_size(axis)
        ends = count - 1
        head = lax.slice_in_dim(cells, 0, width, axis=dim)
        tail = lax.slice_in_dim(cells, cells.shape[dim] - width, cells.shape[dim], axis=dim)
        cells = jnp.concatenate(
            [
                lax.ppermute(tail, axis, [(i, (i + 1) % count) for i in range(ends)]),
                cells,
                lax.ppermute(head, axis, [((i + 1) % count, i) for i in range(ends)]),
            ],
            axis=dim,
        )
    return cells


def per_device(amplitudes, integrals, cd_tiles, tile_counts, eps_occ, eps_virt):
    own_rows = amplitudes.shape[0]
    own_tiles = amplitudes.shape[2]
    slot_count = integrals.shape[1]
    first_tile = lax.axis_index("virt") * own_tiles
    first_row = lax.axis_index("pair") * own_rows
    local_tiles = cd_tiles - first_tile + own_tiles
    slot_ids = lax.broadcasted_iota(jnp.int32, cd_tiles.shape, 1)
    kept_slots = (slot_ids < tile_counts[:, None]).astype(jnp.bfloat16)
    masked_weights = integrals * kept_slots[:, :, None, None]
    padded = extended(amplitudes, (("virt", 2),), own_tiles)
    block_width = min(4, slot_count)
    ladder = None
    for block_start in range(0, slot_count, block_width):
        block_stop = min(block_start + block_width, slot_count)
        columns = local_tiles[:, block_start:block_stop]
        picked = jnp.take(padded, columns, axis=2)
        weights = masked_weights[:, block_start:block_stop]
        term = jnp.einsum("ijasd,asdb->ijab", picked, weights, preferred_element_type=jnp.float32)
        ladder = term if ladder is None else ladder + term
    arrived_ladder = lax.all_to_all(
        lax.all_to_all(ladder, "pair", split_axis=1, concat_axis=0, tiled=True),
        "virt",
        split_axis=3,
        concat_axis=2,
        tiled=True,
    )
    partner = jnp.transpose(arrived_ladder, (1, 0, 3, 2))
    occupied_own = lax.dynamic_slice_in_dim(eps_occ, first_row, own_rows)
    virtual_own = lax.dynamic_slice_in_dim(eps_virt, first_tile, own_tiles)
    denominator = (
        occupied_own[:, None, None, None]
        + eps_occ[None, :, None, None]
        - virtual_own[None, None, :, None]
        - eps_virt[None, None, None, :]
    )
    return ((ladder + partner) / denominator).astype(jnp.bfloat16)


def solution(mesh):
    in_specs = (
        P("pair", None, "virt", None),
        P("virt", None, None, None),
        P("virt", None),
        P("virt"),
        P(),
        P(),
    )
    out_specs = P("pair", None, "virt", None)
    return jax.shard_map(
        per_device, mesh=mesh, in_specs=in_specs, out_specs=out_specs, check_vma=False
    )
```

profile of v0, /device:TPU:15, one launch (start us, length us, event | category | flops | bytes accessed | tf_op | source)
XLA Modules:
  0.0 1326.7 jit_solution(11712600738236134319)
XLA Ops:
  0.0 13.5 %copy.69 = bf16[6,96,64,128]{3,1,2,0:T(8,128)(2,1)} copy(bf16[6,96,64,128]{3,2,1,0:T(8,128)(2,1)} %param.8) | data formatting | bytes 18874368 | tf_op args[0]
  13.5 1.3 collective-permute-start
  14.8 11.7 collective-permute-start.1
  26.5 0.7 subtract_add_fusion
  27.2 0.1 copy.75
  27.3 0.1 reshape.119
  27.4 0.1 copy.78
  27.5 0.1 reshape.123
  27.7 0.1 copy.77
  27.8 0.7 copy.74
  28.5 0.1 copy.81
  28.6 0.1 reshape.127
  28.7 0.1 copy.84
  28.8 0.1 reshape.131
  28.9 0.7 copy.80
  29.6 0.1 copy.72
  29.7 0.1 reshape.115
  29.8 0.7 copy.68
  30.5 0.7 copy.83
  31.2 0.7 fusion.25
  31.9 28.2 %broadcast_multiply_fusion = bf16[64,20,128,128]{3,2,1,0:T(8,128)(2,1)} fusion(bf16[64,20,128,128]{3,2,1,0:T(8,128)(2,1)} %param.9, bf16[64,20]{1,0:T(8,128)(2,1)S(1)} %fusion.25), kind=kLoop, calls=%fused_computation.25 | loop fusion | flops 20971520 | bytes 83888640 | tf_op jit(solution)/shard_map/mul | solution.py:33
  60.2 159.3 %collective-permute-done = bf16[6,96,64,128]{3,1,2,0:T(8,128)(2,1)} collective-permute-done((bf16[6,96,64,128]{3,1,2,0:T(8,128)(2,1)}, bf16[6,96,64,128]{3,1,2,0:T(8,128)(2,1)}, u32[]{:S(2)}, u32[]{:S(2)}) %collective-permute-start) | collective-permute-done | bytes 9437216 | tf_op jit(solution)/shard_map/ppermute | solution.py:15
  219.5 9.0 constant_dynamic-update-slice_fusion.2
  228.5 13.3 %constant_dynamic-update-slice_fusion.1 = bf16[6,96,192,128]{3,1,2,0:T(8,128)(2,1)} fusion(bf16[6,96,192,128]{3,1,2,0:T(8,128)(2,1)} %constant_dynamic-update-slice_fusion.2, bf16[6,96,64,128]{3,2,1,0:T(8,128)(2,1)} %param.8), kind=kLoop, calls=%fused_computation.49 | loop fusion | bytes 18874368
  241.8 9.0 constant_dynamic-update-slice_fusion
  250.8 24.5 %gather_fusion.2 = bf16[256,6,96,128]{3,2,1,0:T(8,128)(2,1)} fusion(bf16[6,96,192,128]{3,1,2,0:T(8,128)(2,1)} %constant_dynamic-update-slice_fusion, s32[1024]{0:T(1024)S(1)} %get-tuple-element.18), kind=kCustom, calls=%fused_computation.2.clone | custom fusion | bytes 75498496 | tf_op jit(solution)/shard_map/jit(_take)/gather | solution.py:40
  275.4 24.4 %gather_fusion.1 = bf16[256,6,96,128]{3,2,1,0:T(8,128)(2,1)} fusion(bf16[6,96,192,128]{3,1,2,0:T(8,128)(2,1)} %constant_dynamic-update-slice_fusion, s32[1024]{0:T(1024)S(1)} %get-tuple-element.19), kind=kCustom, calls=%fused_computation.1.clone | custom fusion | bytes 75498496 | tf_op jit(solution)/shard_map/jit(_take)/gather | solution.py:40
  299.8 24.3 %gather_fusion.3 = bf16[256,6,96,128]{3,2,1,0:T(8,128)(2,1)} fusion(bf16[6,96,192,128]{3,1,2,0:T(8,128)(2,1)} %constant_dynamic-update-slice_fusion, s32[1024]{0:T(1024)S(1)} %get-tuple-element.17), kind=kCustom, calls=%fused_computation.3.clone | custom fusion | bytes 75498496 | tf_op jit(solution)/shard_map/jit(_take)/gather | solution.py:40
  324.1 24.3 %gather_fusion = bf16[256,6,96,128]{3,2,1,0:T(8,128)(2,1)} fusion(bf16[6,96,192,128]{3,1,2,0:T(8,128)(2,1)} %constant_dynamic-update-slice_fusion, s32[1024]{0:T(1024)S(1)} %pad_clamp_fusion.4), kind=kCustom, calls=%fused_computation.clone | custom fusion | bytes 75498496 | tf_op jit(solution)/shard_map/jit(_take)/gather | solution.py:40
  348.4 24.4 %gather_fusion.4 = bf16[256,6,96,128]{3,2,1,0:T(8,128)(2,1)} fusion(bf16[6,96,192,128]{3,1,2,0:T(8,128)(2,1)} %constant_dynamic-update-slice_fusion, s32[1024]{0:T(1024)S(1)} %get-tuple-element.16), kind=kCustom, calls=%fused_computation.4.clone | custom fusion | bytes 75498496 | tf_op jit(solution)/shard_map/jit(_take)/gather | solution.py:40
  372.8 22.9 %fusion.4 = f32[64,128,6,96,1]{1,3,4,2,0:T(8,128)} fusion(bf16[64,4,6,96,128]{4,3,2,1,0:T(8,128)(2,1)} %bitcast.110, pred[64,4]{1,0:T(8,128)(4,1)S(1)} %copy.77, bf16[64,20,128,128]{3,2,1,0:T(8,128)(2,1)} %broadcast_multiply_fusion), kind=kOutput, calls=%fused_computation.9 | convolution fusion | flops 4850712576 | bytes 65011968 | tf_op jit(solution)/shard_map/ijasd,asdb->ijab/dot_general | solution.py:42
  395.7 22.8 %fusion.6 = f32[64,128,6,96,1]{1,3,4,2,0:T(8,128)} fusion(bf16[64,4,6,96,128]{4,3,2,1,0:T(8,128)(2,1)} %bitcast.111, pred[64,4]{1,0:T(8,128)(4,1)S(1)} %copy-done.1, bf16[64,20,128,128]{3,2,1,0:T(8,128)(2,1)} %broadcast_multiply_fusion), kind=kOutput, calls=%fused_computation.11 | convolution fusion | flops 4850712576 | bytes 65011968 | tf_op jit(solution)/shard_map/ijasd,asdb->ijab/dot_general | solution.py:42
  418.5 23.0 %fusion.2 = f32[64,128,6,96,1]{1,3,4,2,0:T(8,128)} fusion(bf16[64,4,6,96,128]{4,3,2,1,0:T(8,128)(2,1)} %bitcast.109, pred[64,4]{1,0:T(8,128)(4,1)S(1)} %copy-done.2, bf16[64,20,128,128]{3,2,1,0:T(8,128)(2,1)} %broadcast_multiply_fusion), kind=kOutput, calls=%fused_computation.7 | convolution fusion | flops 4850712576 | bytes 65011968 | tf_op jit(solution)/shard_map/ijasd,asdb->ijab/dot_general | solution.py:42
  441.4 22.8 %fusion.8 = f32[64,128,6,96,1]{1,3,4,2,0:T(8,128)} fusion(bf16[64,4,6,96,128]{4,3,2,1,0:T(8,128)(2,1)} %bitcast.108, pred[64,4]{1,0:T(8,128)(4,1)S(1)} %copy-done.3, bf16[64,20,128,128]{3,2,1,0:T(8,128)(2,1)} %broadcast_multiply_fusion), kind=kOutput, calls=%fused_computation.13 | convolution fusion | flops 4850712576 | bytes 65011968 | tf_op jit(solution)/shard_map/ijasd,asdb->ijab/dot_general | solution.py:42
  464.2 45.3 %fusion.17 = f32[6,96,64,128]{3,1,0,2:T(8,128)} fusion(f32[64,128,6,96,1]{1,3,4,2,0:T(8,128)} %fusion.2, f32[64,128,6,96,1]{1,3,4,2,0:T(8,128)} %fusion.4, f32[64,128,6,96,1]{1,3,4,2,0:T(8,128)} %fusion.6, f32[64,128,6,96,1]{1,3,4,2,0:T(8,128)} %fusion.8, bf16[64,4,6,96,128]{4,3,2,1,0:T(8,128)(2,1)} %bitcast.104, pred[64,4]{1,0:T(8,128)(4,1)S(1)} %copy-done, ...), kind=kOutput, calls=%fused_computation.30 | convolution fusion | flops 4869586944 | bytes 140509440 | tf_op jit(solution)/shard_map/ijasd,asdb->ijab/dot_general | solution.py:42
  509.5 12.4 copy.86
  521.9 414.0 %all_to_all.36 = f32[6,96,64,128]{3,2,0,1:T(8,128)S(1)} all-to-all(f32[6,96,64,128]{3,2,0,1:T(8,128)S(1)} %copy.86), channel_id=1, replica_groups=mesh['pair'=16,'virt'=2] {'pair'}, dimensions={1} | all-to-all | bytes 37748736 | tf_op jit(solution)/shard_map/all_to_all | solution.py:45
  935.9 7.4 copy.88
  943.4 22.8 %copy.89 = f32[96,6,64,128]{0,2,1,3:T(8,128)} copy(f32[96,6,64,128]{3,2,1,0:T(8,128)} %bitcast.107) | data formatting | bytes 37748736 | tf_op jit(solution)/shard_map/all_to_all | solution.py:45
  966.2 11.8 all-to-all-start.1
  978.0 0.1 dynamic_slice.7
  978.1 0.1 dynamic_slice.6
  978.3 0.1 broadcast_subtract_fusion
  978.4 269.8 %all-to-all-done.1 = f32[96,6,64,128]{0,2,1,3:T(8,128)} async-done(((f32[96,6,64,128]{0,2,1,3:T(8,128)}), f32[96,6,64,128]{0,2,1,3:T(8,128)}, u32[]{:S(2)}, u32[]{:S(2)}) %all-to-all-start.1) | async-done | bytes 18874400 | tf_op jit(solution)/shard_map/all_to_all | solution.py:44
  1248.2 25.0 %copy.91 = f32[96,6,2,64,64]{0,4,3,2,1:T(8,128)} copy(f32[96,6,2,64,64]{0,3,1,4,2:T(8,128)} %bitcast.37) | data formatting | bytes 37748736 | tf_op jit(solution)/shard_map/all_to_all | solution.py:44
  1273.2 22.6 %copy.92 = f32[96,6,128,64]{2,0,1,3:T(8,128)} copy(f32[96,6,128,64]{0,3,2,1:T(8,128)} %bitcast.105) | data formatting | bytes 37748736 | tf_op jit(solution)/shard_map/all_to_all | solution.py:44
  1295.8 16.9 %fusion.16 = bf16[6,96,64,128]{3,1,0,2:T(8,128)(2,1)} fusion(f32[6,96,64,128]{3,1,0,2:T(8,128)} %fusion.17, f32[96,6,128,64]{2,0,1,3:T(8,128)} %copy.92, f32[128]{0:T(128)S(1)} %copy-done.4, f32[6,96,64]{1,0,2:T(8,128)S(1)} %broadcast_subtract_fusion), kind=kLoop, calls=%fused_computation.28 | loop fusion | flops 18874368 | bytes 47333888 | tf_op jit(solution)/shard_map/convert_element_type | solution.py:60
  1312.7 13.5 %copy.93 = bf16[6,96,64,128]{3,2,1,0:T(8,128)(2,1)} copy(bf16[6,96,64,128]{3,1,0,2:T(8,128)(2,1)} %fusion.16) | data formatting | bytes 18874368 | tf_op jit(solution)/shard_map/convert_element_type | solution.py:60
  (19 shorter events, 0.1 us)
Async XLA Ops:
  13.5 206.0 %collective-permute-start = (bf16[6,96,64,128]{3,1,2,0:T(8,128)(2,1)}, bf16[6,96,64,128]{3,1,2,0:T(8,128)(2,1)}, u32[]{:S(2)}, u32[]{:S(2)}) collective-permute-start(bf16[6,96,64,128]{3,1,2,0:T(8,128)(2,1)} %copy.69), channel_id=1, source_target_pairs={{0,1},{2,3},{4,5},{6,7},{8,9},{10,11},{12,13},{14,15},{16,17},{18,... | collective-permute-start | bytes 28311560 | tf_op jit(solution)/shard_map/ppermute | solution.py:15
  14.8 227.0 %collective-permute-start.1 = (bf16[6,96,64,128]{3,1,2,0:T(8,128)(2,1)}, bf16[6,96,64,128]{3,1,2,0:T(8,128)(2,1)}, u32[]{:S(2)}, u32[]{:S(2)}) collective-permute-start(bf16[6,96,64,128]{3,1,2,0:T(8,128)(2,1)} %copy.69), channel_id=1, source_target_pairs={{1,0},{3,2},{5,4},{7,6},{9,8},{11,10},{13,12},{15,14},{17,16},{19,... | collective-permute-start | bytes 28311560 | tf_op jit(solution)/shard_map/ppermute | solution.py:17
  372.8 22.9 %copy-start.1 = (pred[64,4]{1,0:T(8,128)(4,1)S(1)}, pred[64,4]{1,0:T(8,128)(4,1)}, u32[]{:S(2)}) copy-start(pred[64,4]{1,0:T(8,128)(4,1)} %copy.74) | copy-start | bytes 772
  395.7 22.8 %copy-start.2 = (pred[64,4]{1,0:T(8,128)(4,1)S(1)}, pred[64,4]{1,0:T(8,128)(4,1)}, u32[]{:S(2)}) copy-start(pred[64,4]{1,0:T(8,128)(4,1)} %copy.80) | copy-start | bytes 772
  418.5 23.0 %copy-start.3 = (pred[64,4]{1,0:T(8,128)(4,1)S(1)}, pred[64,4]{1,0:T(8,128)(4,1)}, u32[]{:S(2)}) copy-start(pred[64,4]{1,0:T(8,128)(4,1)} %copy.68) | copy-start | bytes 772
  441.4 22.8 %copy-start = (pred[64,4]{1,0:T(8,128)(4,1)S(1)}, pred[64,4]{1,0:T(8,128)(4,1)}, u32[]{:S(2)}) copy-start(pred[64,4]{1,0:T(8,128)(4,1)} %copy.83) | copy-start | bytes 772
  966.2 11.9 copy-start.4
  966.2 11.9 copy-start.5
  966.2 282.0 %all-to-all-start.1 = ((f32[96,6,64,128]{0,2,1,3:T(8,128)}), f32[96,6,64,128]{0,2,1,3:T(8,128)}, u32[]{:S(2)}, u32[]{:S(2)}) async-start(f32[96,6,64,128]{0,2,1,3:T(8,128)} %copy.89), calls=%async_computation.1 | async-start | bytes 50331648 | tf_op jit(solution)/shard_map/all_to_all | solution.py:44
where the time goes:
time: 1340 us; the launch traced here: 1330 us
  waiting for transfers between devices  429 us (32%)
  blocking collectives  414 us (31%)
  local copies, waits for them, and re-layouts  275 us (21%)
  matrix products  137 us (10%)
  other arithmetic  46.8 us (3%)
  starting transfers between devices  24.8 us (2%)
    all_to_all x1, blocking collectives, per_device(): lax.all_to_all(ladder, 'pair', split_axis=1, concat_axis=0, tiled=True)  414 us
    all_to_all x1, waiting for transfers between devices, per_device(): lax.all_to_all(lax.all_to_all(ladder, 'pair', split_axis=1, concat_axis=0...  270 us
    ppermute x1, waiting for transfers between devices, extended(): lax.ppermute(tail, axis, [(i, (i + 1) % count) for i in range(ends)])  159 us
    dot_general x5, matrix products, per_device(): jnp.einsum('ijasd,asdb->ijab', picked, weights, preferred_element_type=jn...  137 us
    gather x5, local copies, waits for them, and re-layouts, per_device(): picked = jnp.take(padded, columns, axis=2)  122 us
    all_to_all x2, local copies, waits for them, and re-layouts, per_device(): lax.all_to_all(lax.all_to_all(ladder, 'pair', split_axis=1, concat_axis=0...  47.6 us
    unnamed x15, local copies, waits for them, and re-layouts  35.8 us
    all_to_all x2, local copies, waits for them, and re-layouts, per_device(): lax.all_to_all(ladder, 'pair', split_axis=1, concat_axis=0, tiled=True)  30.3 us
  transfers between devices with their start and end apart: 3, of which 2 were waited for; matrix products, arithmetic and copies ran while one was open for 4% of the time, Pallas kernels for 0%

commit v1 on v0

--- a/solution.py
+++ b/solution.py
@@ -1,7 +1,16 @@
+import functools
+
 import jax
 import jax.numpy as jnp
 from jax import lax
+from jax.experimental import pallas as pl
+from jax.experimental.pallas import tpu as pltpu
 from jax.sharding import PartitionSpec as P
+
+MESH = pl.DeviceIdType.MESH
+CHUNKS = 3
+GROUP = 4
+TOP = 32767.0
 
 
 def extended(cells, sides, width):
@@ -21,7 +30,7 @@
     return cells
 
 
-def per_device(amplitudes, integrals, cd_tiles, tile_counts, eps_occ, eps_virt):
+def general_device(amplitudes, integrals, cd_tiles, tile_counts, eps_occ, eps_virt):
     own_rows = amplitudes.shape[0]
     own_tiles = amplitudes.shape[2]
     slot_count = integrals.shape[1]
@@ -60,6 +69,271 @@
     return ((ladder + partner) / denominator).astype(jnp.bfloat16)
 
 
+def ladder_kernel(pairs, tiles, loops, own, other, weights, ladder, codes, scales, picked, sems):
+    k, h, s = pl.program_id(0), pl.program_id(1), pl.program_id(2)
+    steps, halves, eight = pl.num_programs(0), pl.num_programs(1), pl.num_programs(2)
+    held = own.shape[0]
+    rows, depth = own.shape[1], own.shape[2]
+    wide = ladder.shape[3]
+    half = wide // 2
+
+    @pl.when((k == 0) & (h == 0) & (s == 0))
+    def _():
+        first = pltpu.make_async_copy(own, picked.at[pl.ds(0, held)], sems.at[0])
+        second = pltpu.make_async_copy(other, picked.at[pl.ds(held, held)], sems.at[1])
+        first.start()
+        second.start()
+        picked[2 * held] = jnp.zeros((rows, depth), picked.dtype)
+        first.wait()
+        second.wait()
+
+    a = (h * steps + k) * eight + s
+
+    def add(g, total):
+        lhs = jnp.concatenate([picked[tiles[a, g * GROUP + x]] for x in range(GROUP)], axis=1)
+        rhs = weights[0, pl.ds(g * GROUP, GROUP)].reshape(GROUP * depth, wide)
+        return total + jnp.dot(lhs, rhs, preferred_element_type=jnp.float32)
+
+    total = lax.fori_loop(0, loops[a], add, jnp.zeros((rows, wide), jnp.float32))
+    ladder[h, 0, pl.ds(s, rows, stride=8), :] = total
+
+    @pl.when((h == halves - 1) & (s == eight - 1))
+    def _():
+        tall = codes.shape[3]
+        low = lax.broadcasted_iota(jnp.int32, (tall, wide), 1) < half
+
+        def largest(p, tops):
+            spot = pl.ds(pl.multiple_of(p * tall, 8), tall)
+            return tuple(
+                jnp.maximum(
+                    top,
+                    jnp.max(jnp.abs(ladder[x, 0, spot, :]).reshape(tall // 8, 8, wide), axis=0),
+                )
+                for x, top in enumerate(tops)
+            )
+
+        tops = lax.fori_loop(0, pairs, largest, (jnp.zeros((8, wide), jnp.float32),) * 2)
+        tops = [jnp.maximum(jnp.max(top, axis=0, keepdims=True), 1e-30) for top in tops]
+        sizes = [top / TOP for top in tops]
+        factors = [TOP / top for top in tops]
+        low_row = low[:1]
+        scales[0, pl.ds(k, 1), :] = jnp.where(low_row, sizes[0], pltpu.roll(sizes[1], half, 1))
+        scales[1, pl.ds(k, 1), :] = jnp.where(low_row, pltpu.roll(sizes[0], half, 1), sizes[1])
+
+        def pack(p, _):
+            spot = pl.ds(pl.multiple_of(p * tall, 8), tall)
+            zero, one = (jnp.round(ladder[x, 0, spot, :] * factors[x]) for x in range(2))
+            left = jnp.where(low, zero, pltpu.roll(one, half, 1))
+            right = jnp.where(low, pltpu.roll(zero, half, 1), one)
+            codes[p, 0, 0] = left.astype(jnp.int32).astype(jnp.int16)
+            codes[p, 1, 0] = right.astype(jnp.int32).astype(jnp.int16)
+            return 0
+
+        lax.fori_loop(0, pairs, pack, 0)
+
+
+def exchange_kernel(pairs, virts, codes, scales, arrived, sizes, send, recv, send_s, recv_s, own):
+    mine_p, mine_v = lax.axis_index("pair"), lax.axis_index("virt")
+    me = mine_p * virts + mine_v
+    count = pairs * virts
+    barrier = pltpu.get_barrier_semaphore()
+
+    def target(d):
+        t = lax.rem(me + d, count)
+        return t // virts, lax.rem(t, virts)
+
+    def greet(d, _):
+        p, v = target(d)
+        pl.semaphore_signal(barrier, inc=1, device_id=(p, v), device_id_type=MESH)
+        return 0
+
+    lax.fori_loop(1, count, greet, 0)
+    keep = pltpu.make_async_copy(codes.at[mine_p, mine_v], arrived.at[mine_p, mine_v], own.at[0])
+    keep_s = pltpu.make_async_copy(scales.at[mine_v], sizes.at[mine_p, mine_v], own.at[1])
+    keep.start()
+    keep_s.start()
+    pl.semaphore_wait(barrier, count - 1)
+
+    def copies(d):
+        p, v = target(d)
+        return (
+            pltpu.make_async_remote_copy(
+                src_ref=codes.at[p, v],
+                dst_ref=arrived.at[mine_p, mine_v],
+                send_sem=send.at[d],
+                recv_sem=recv.at[d],
+                device_id=(p, v),
+                device_id_type=MESH,
+            ),
+            pltpu.make_async_remote_copy(
+                src_ref=scales.at[v],
+                dst_ref=sizes.at[mine_p, mine_v],
+                send_sem=send_s.at[d],
+                recv_sem=recv_s.at[d],
+                device_id=(p, v),
+                device_id_type=MESH,
+            ),
+        )
+
+    def begin(d, _):
+        for copy in copies(d):
+            copy.start()
+        return 0
+
+    def finish(d, _):
+        for copy in copies(d):
+            copy.wait()
+        return 0
+
+    lax.fori_loop(1, count, begin, 0)
+    lax.fori_loop(1, count, finish, 0)
+    keep.wait()
+    keep_s.wait()
+
+
+def combine_kernel(chunks, rows, *refs):
+    occ_own, occ_all, virt_own, virt_all = refs[:4]
+    ladders = refs[4 : 4 + chunks]
+    codes = refs[4 + chunks : 4 + 2 * chunks]
+    scales = refs[4 + 2 * chunks : 4 + 3 * chunks]
+    out = refs[4 + 3 * chunks]
+    values = refs[5 + 3 * chunks]
+    p = pl.program_id(0)
+    virts, steps, tall, wide = codes[0].shape[1:]
+    part = rows // chunks
+    quarter = steps * 8
+    half = wide // 2
+    for r in range(chunks):
+        for v in range(virts):
+            for k in range(steps):
+                values[r, v, k] = codes[r][0, v, k].astype(jnp.float32) * scales[r][0, v, k : k + 1, :]
+    low = virt_own[...] + virt_all[...]
+    for jj in range(rows):
+        chunk, inner = jj // part, jj % part
+        for i in range(rows):
+            spot = pl.ds((inner * rows + i) * 8, 8)
+            tile = values[chunk, :, :, spot, :].reshape(virts * quarter, wide)
+            turned = tile.T
+            partner = jnp.concatenate(
+                [
+                    turned[x * half : (x + 1) * half, v * quarter : (v + 1) * quarter]
+                    for v in range(virts)
+                    for x in range(2)
+                ],
+                axis=1,
+            )
+            here = pl.ds(((i % part) * rows + jj) * 8, 8)
+            mine = ladders[i // part][:, :, 0, here, :].reshape(2 * quarter, wide)
+            level = occ_own[i] + occ_all[p * rows + jj]
+            out[i, jj] = ((mine + partner) / (level - low)).astype(out.dtype)
+
+
+def per_device(amplitudes, integrals, cd_tiles, tile_counts, eps_occ, eps_virt):
+    pairs, virts = lax.axis_size("pair"), lax.axis_size("virt")
+    rows, others, held, depth = amplitudes.shape
+    slots, wide = integrals.shape[1], integrals.shape[3]
+    fits = virts == 2 and held % 16 == 0 and rows % CHUNKS == 0 and slots % GROUP == 0
+    fits = fits and wide == 2 * held and wide == 128 and (rows // CHUNKS * rows) % 2 == 0
+    if not fits:
+        return general_device(amplitudes, integrals, cd_tiles, tile_counts, eps_occ, eps_virt)
+    part = rows // CHUNKS
+    block = part * rows
+    count = pairs * block
+    tall = block * 8
+    steps = held // 16
+    first_tile = lax.axis_index("virt") * held
+    first_row = lax.axis_index("pair") * rows
+    slot_ids = lax.broadcasted_iota(jnp.int32, cd_tiles.shape, 1)
+    places = lax.rem(cd_tiles - first_tile + 2 * held, 2 * held)
+    tiles = jnp.where(slot_ids < tile_counts[:, None], places, 2 * held)
+    loops = (tile_counts + GROUP - 1) // GROUP
+
+    ladders, arrived, sizes = [], [], []
+    swapped = []
+    for r in range(CHUNKS):
+        own = amplitudes[r * part : (r + 1) * part].reshape(part, pairs, rows, held, depth)
+        own = jnp.transpose(own, (3, 1, 0, 2, 4)).reshape(held, count, depth)
+        swapped.append((own, lax.ppermute(own, "virt", [(0, 1), (1, 0)])))
+    for r in range(CHUNKS):
+        own, other = swapped[r]
+        ladder, codes, scale = pl.pallas_call(
+            functools.partial(ladder_kernel, pairs),
+            grid_spec=pltpu.PrefetchScalarGridSpec(
+                num_scalar_prefetch=2,
+                grid=(steps, 2, 8),
+                in_specs=[
+                    pl.BlockSpec(memory_space=pl.ANY),
+                    pl.BlockSpec(memory_space=pl.ANY),
+                    pl.BlockSpec(
+                        (1, slots, depth, wide),
+                        lambda k, h, s, *_: ((h * steps + k) * 8 + s, 0, 0, 0),
+                    ),
+                ],
+                out_specs=[
+                    pl.BlockSpec((2, 1, count * 8, wide), lambda k, h, s, *_: (0, k, 0, 0)),
+                    pl.BlockSpec((pairs, 2, 1, tall, wide), lambda k, h, s, *_: (0, 0, k, 0, 0)),
+                    pl.BlockSpec((2, 8, wide), lambda k, h, s, *_: (0, 0, 0)),
+                ],
+                scratch_shapes=[
+                    pltpu.VMEM((2 * held + 1, count, depth), amplitudes.dtype),
+                    pltpu.SemaphoreType.DMA((2,)),
+                ],
+            ),
+            out_shape=[
+                jax.ShapeDtypeStruct((2, steps, count * 8, wide), jnp.float32),
+                jax.ShapeDtypeStruct((pairs, 2, steps, tall, wide), jnp.int16),
+                jax.ShapeDtypeStruct((2, 8, wide), jnp.float32),
+            ],
+            cost_estimate=pl.CostEstimate(
+                flops=2 * count * held * slots * depth * wide,
+                bytes_accessed=2 * integrals.size,
+                transcendentals=0,
+            ),
+            compiler_params=pltpu.CompilerParams(vmem_limit_bytes=60 * 2**20),
+            name=f"ladder_{r}",
+        )(tiles, loops, own, other, integrals)
+        got, size = pl.pallas_call(
+            functools.partial(exchange_kernel, pairs, virts),
+            in_specs=[pl.BlockSpec(memory_space=pl.ANY)] * 2,
+            out_specs=[pl.BlockSpec(memory_space=pl.ANY)] * 2,
+            out_shape=[
+                jax.ShapeDtypeStruct(codes.shape, codes.dtype),
+                jax.ShapeDtypeStruct((pairs,) + scale.shape, scale.dtype),
+            ],
+            scratch_shapes=[pltpu.SemaphoreType.DMA((pairs * virts,))] * 4
+            + [pltpu.SemaphoreType.DMA((2,))],
+            compiler_params=pltpu.CompilerParams(collective_id=r, has_side_effects=True),
+            name=f"exchange_{r}",
+        )(codes, scale)
+        ladders.append(ladder.reshape(2, steps, pairs, tall, wide))
+        arrived.append(got)
+        sizes.append(size)
+    occ_own = lax.dynamic_slice_in_dim(eps_occ, first_row, rows)
+    virt_own = lax.dynamic_slice_in_dim(eps_virt, first_tile, held)
+    smem = pl.BlockSpec(memory_space=pltpu.SMEM)
+    vmem = pl.BlockSpec(memory_space=pltpu.VMEM)
+    return pl.pallas_call(
+        functools.partial(combine_kernel, CHUNKS, rows),
+        grid=(pairs,),
+        in_specs=[smem, smem, vmem, vmem]
+        + [pl.BlockSpec((2, steps, 1, tall, wide), lambda p: (0, 0, p, 0, 0))] * CHUNKS
+        + [pl.BlockSpec((1, 2, steps, tall, wide), lambda p: (p, 0, 0, 0, 0))] * CHUNKS
+        + [pl.BlockSpec((1, 2, 8, wide), lambda p: (p, 0, 0, 0))] * CHUNKS,
+        out_specs=pl.BlockSpec((rows, rows, held, wide), lambda p: (0, p, 0, 0)),
+        out_shape=jax.ShapeDtypeStruct(amplitudes.shape[:3] + (wide,), jnp.bfloat16),
+        scratch_shapes=[pltpu.VMEM((CHUNKS, 2, steps, tall, wide), jnp.float32)],
+        name="combine",
+    )(
+        occ_own,
+        eps_occ,
+        jnp.broadcast_to(virt_own[:, None], (held, wide)),
+        jnp.broadcast_to(eps_virt[None, :], (held, wide)),
+        *ladders,
+        *arrived,
+        *sizes,
+    )
+
+
 def solution(mesh):
     in_specs = (
         P("pair", None, "virt", None),

time: 1340 us -> 606 us (0.45)
  Pallas kernels: 0 us -> 523 us
  blocking collectives: 414 us -> 0 us
  waiting for transfers between devices: 429 us -> 58.1 us
  local copies, waits for them, and re-layouts: 275 us -> 18.7 us
  matrix products: 137 us -> 0 us
  other arithmetic: 46.8 us -> 1.23 us
  starting transfers between devices: 24.8 us -> 1.76 us
    pallas_call x0 -> x7, Pallas kernels: none -> 523 us  [the longest x3 252 us: per_device(): pl.pallas_call(functools.partial(exchange_kernel, pairs, virts), in_specs...]
    all_to_all x1 -> x0, blocking collectives: 414 us -> none  [per_device(): lax.all_to_all(ladder, 'pair', split_axis=1, concat_axis=0, tiled=True)]
    all_to_all x1 -> x0, waiting for transfers between devices: 270 us -> none  [per_device(): lax.all_to_all(lax.all_to_all(ladder, 'pair', split_axis=1, concat_axis=0...]
    dot_general x5 -> x0, matrix products: 137 us -> none  [per_device(): jnp.einsum('ijasd,asdb->ijab', picked, weights, preferred_element_type=jn...]
    gather x5 -> x0, local copies, waits for them, and re-layouts: 122 us -> none  [per_device(): picked = jnp.take(padded, columns, axis=2)]
    ppermute x2 -> x3, waiting for transfers between devices: 159 us -> 58.1 us  [per_device(): swapped.append((own, lax.ppermute(own, 'virt', [(0, 1), (1, 0)])))]
    all_to_all x4 -> x0, local copies, waits for them, and re-layouts: 77.8 us -> none  [the longest x2 47.6 us: per_device(): lax.all_to_all(lax.all_to_all(ladder, 'pair', split_axis=1, concat_axis=0...]
    unnamed x15 -> x11, local copies, waits for them, and re-layouts: 35.8 us -> 0.12 us
  transfers between devices with their start and end apart: 3 -> 3, of which waited for: 2 -> 1; matrix products, arithmetic and copies ran while one was open for 4% -> 2% of each run, Pallas kernels for 0% -> 55%
where the time goes in v1:
time: 606 us; the launch traced here: 602 us
  Pallas kernels  523 us (86%)
  waiting for transfers between devices  58.1 us (10%)
  local copies, waits for them, and re-layouts  18.7 us (3%)
    pallas_call x3, Pallas kernels, per_device(): pl.pallas_call(functools.partial(exchange_kernel, pairs, virts), in_specs...  252 us
    pallas_call x3, Pallas kernels, per_device(): pl.pallas_call(functools.partial(ladder_kernel, pairs), grid_spec=pltpu.P...  241 us
    ppermute x3, waiting for transfers between devices, per_device(): swapped.append((own, lax.ppermute(own, 'virt', [(0, 1), (1, 0)])))  58.1 us
    pallas_call x1, Pallas kernels, per_device(): pl.pallas_call(functools.partial(combine_kernel, CHUNKS, rows), grid=(pai...  29.3 us
  transfers between devices with their start and end apart: 3, of which 1 were waited for; matrix products, arithmetic and copies ran while one was open for 2% of the time, Pallas kernels for 55%

profile of v1, /device:TPU:15, one launch (start us, length us, event | category | flops | bytes accessed | tf_op | source)
XLA Modules:
  0.0 602.5 jit_solution(854680197231196553)
XLA Ops:
  0.0 4.8 fusion.2
  4.9 0.7 copy.25
  5.6 3.7 copy.27.own
  9.3 0.2 collective-permute-start.2
  9.5 0.7 copy.19
  10.2 3.7 copy.21.own
  13.9 1.2 collective-permute-start
  15.1 0.7 copy.22
  15.8 0.0 copy-start.1
  15.8 0.0 copy-start.4
  15.9 0.0 copy-start.3
  15.9 0.0 copy-start.2
  15.9 2.0 copy.24.own
  17.9 0.0 copy-start
  17.9 0.3 collective-permute-start.1
  18.2 0.0 copy-done.1
  18.2 0.1 copy.18
  18.3 0.0 copy-done.4
  18.3 0.9 dynamic_slice.6.refs_0_
  19.2 0.0 copy-done.3
  19.2 0.1 dynamic_slice.7
  19.3 0.0 copy-done.2
  19.3 0.5 and_select_fusion.loops
  19.8 0.7 fusion.1.tiles
  20.5 58.1 %collective-permute-done.2.other = bf16[64,192,128]{2,1,0:T(8,128)(2,1)} collective-permute-done((bf16[64,192,128]{2,1,0:T(8,128)(2,1)}, bf16[64,192,128]{2,1,0:T(8,128)(2,1)}, u32[]{:S(2)}, u32[]{:S(2)}) %collective-permute-start.2) | collective-permute-done | bytes 3145760 | tf_op jit(solution)/shard_map/ppermute | solution.py:256
  78.6 80.2 %ladder_2.1 = (f32[2,4,1536,128]{3,2,1,0:T(8,128)}, s16[16,2,4,96,128]{4,3,2,1,0:T(8,128)(2,1)}, f32[2,8,128]{2,1,0:T(8,128)}) custom-call(s32[64,20]{1,0:T(8,128)} %fusion.1.tiles, s32[64]{0:T(128)} %and_select_fusion.loops, bf16[64,192,128]{2,1,0:T(8,128)(2,1)} %copy.27.own, bf16[64,192,128]{2,1,0:T(8,128)(2,1)} %collective-permute-done.2.other, ...), custom_call_target="tpu_custom_call" | custom-call | flops 8053063680 | bytes 41943040 | tf_op jit(solution)/shard_map/ladder_2/pallas_call | solution.py:259
  158.8 0.0 copy-done
  158.9 91.9 %exchange_2.1 = (s16[16,2,4,96,128]{4,3,2,1,0:T(8,128)(2,1)}, f32[16,2,8,128]{3,2,1,0:T(8,128)}) custom-call(s16[16,2,4,96,128]{4,3,2,1,0:T(8,128)(2,1)} %get-tuple-element.29.codes, f32[2,8,128]{2,1,0:T(8,128)} %get-tuple-element.30.scales), custom_call_target="tpu_custom_call" | custom-call | tf_op jit(solution)/shard_map/exchange_2/pallas_call | solution.py:295
  250.8 0.0 collective-permute-done.other
  250.8 80.3 %ladder_0.1 = (f32[2,4,1536,128]{3,2,1,0:T(8,128)}, s16[16,2,4,96,128]{4,3,2,1,0:T(8,128)(2,1)}, f32[2,8,128]{2,1,0:T(8,128)}) custom-call(s32[64,20]{1,0:T(8,128)} %fusion.1.tiles, s32[64]{0:T(128)} %and_select_fusion.loops, bf16[64,192,128]{2,1,0:T(8,128)(2,1)} %copy.21.own, bf16[64,192,128]{2,1,0:T(8,128)(2,1)} %collective-permute-done.other, ...), custom_call_target="tpu_custom_call" | custom-call | flops 8053063680 | bytes 41943040 | tf_op jit(solution)/shard_map/ladder_0/pallas_call | solution.py:259
  331.1 80.8 %exchange_0.1 = (s16[16,2,4,96,128]{4,3,2,1,0:T(8,128)(2,1)}, f32[16,2,8,128]{3,2,1,0:T(8,128)}) custom-call(s16[16,2,4,96,128]{4,3,2,1,0:T(8,128)(2,1)} %get-tuple-element.23.codes, f32[2,8,128]{2,1,0:T(8,128)} %get-tuple-element.24.scales), custom_call_target="tpu_custom_call" | custom-call | tf_op jit(solution)/shard_map/exchange_0/pallas_call | solution.py:295
  411.9 0.0 collective-permute-done.1.other
  411.9 80.2 %ladder_1.1 = (f32[2,4,1536,128]{3,2,1,0:T(8,128)}, s16[16,2,4,96,128]{4,3,2,1,0:T(8,128)(2,1)}, f32[2,8,128]{2,1,0:T(8,128)}) custom-call(s32[64,20]{1,0:T(8,128)} %fusion.1.tiles, s32[64]{0:T(128)} %and_select_fusion.loops, bf16[64,192,128]{2,1,0:T(8,128)(2,1)} %copy-done, bf16[64,192,128]{2,1,0:T(8,128)(2,1)} %collective-permute-done.1.other, ...), custom_call_target="tpu_custom_call" | custom-call | flops 8053063680 | bytes 41943040 | tf_op jit(solution)/shard_map/ladder_1/pallas_call | solution.py:259
  492.2 79.7 %exchange_1.1 = (s16[16,2,4,96,128]{4,3,2,1,0:T(8,128)(2,1)}, f32[16,2,8,128]{3,2,1,0:T(8,128)}) custom-call(s16[16,2,4,96,128]{4,3,2,1,0:T(8,128)(2,1)} %get-tuple-element.26.codes, f32[2,8,128]{2,1,0:T(8,128)} %get-tuple-element.27.scales), custom_call_target="tpu_custom_call" | custom-call | tf_op jit(solution)/shard_map/exchange_1/pallas_call | solution.py:295
  571.9 0.7 broadcast_in_dim.6.refs_2_
  572.5 0.6 broadcast_in_dim.7.refs_3_
  573.1 29.3 %combine.1 = bf16[6,96,64,128]{3,2,1,0:T(8,128)(2,1)} custom-call(f32[6]{0:T(128)} %dynamic_slice.6.refs_0_, f32[96]{0:T(128)} %refs_1_.1, f32[64,128]{1,0:T(8,128)} %broadcast_in_dim.6.refs_2_, f32[64,128]{1,0:T(8,128)} %broadcast_in_dim.7.refs_3_, f32[2,4,16,96,128]{4,3,2,1,0:T(8,128)} %bitcast.22, f32[2,4,16,96,128]{4,3,2,1,0:T(8,128)} %bitcast.23, ...), custom_call_target="tpu_custom_call" | custom-call | tf_op jit(solution)/shard_map/combine/pallas_call | solution.py:315
Async XLA Ops:
  9.3 69.3 %collective-permute-start.2 = (bf16[64,192,128]{2,1,0:T(8,128)(2,1)}, bf16[64,192,128]{2,1,0:T(8,128)(2,1)}, u32[]{:S(2)}, u32[]{:S(2)}) collective-permute-start(bf16[64,192,128]{2,1,0:T(8,128)(2,1)} %copy.27.own), channel_id=1, source_target_pairs={{0,1},{1,0},{2,3},{3,2},{4,5},{5,4},{6,7},{7,6},{8,9},{9,8},{10,11... | collective-permute-start | bytes 9437192 | tf_op jit(solution)/shard_map/ppermute | solution.py:256
  13.9 236.9 %collective-permute-start = (bf16[64,192,128]{2,1,0:T(8,128)(2,1)}, bf16[64,192,128]{2,1,0:T(8,128)(2,1)}, u32[]{:S(2)}, u32[]{:S(2)}) collective-permute-start(bf16[64,192,128]{2,1,0:T(8,128)(2,1)} %copy.21.own), channel_id=1, source_target_pairs={{0,1},{1,0},{2,3},{3,2},{4,5},{5,4},{6,7},{7,6},{8,9},{9,8},{10,11... | collective-permute-start | bytes 9437192 | tf_op jit(solution)/shard_map/ppermute | solution.py:256
  15.8 2.4 copy-start.1
  15.8 2.5 copy-start.4
  15.9 3.3 copy-start.3
  15.9 3.4 copy-start.2
  17.9 140.9 %copy-start = (bf16[64,192,128]{2,1,0:T(8,128)(2,1)}, bf16[64,192,128]{2,1,0:T(8,128)(2,1)S(1)}, u32[]{:S(2)}) copy-start(bf16[64,192,128]{2,1,0:T(8,128)(2,1)S(1)} %copy.24.own) | copy-start | bytes 9437188
  17.9 394.0 %collective-permute-start.1 = (bf16[64,192,128]{2,1,0:T(8,128)(2,1)S(1)}, bf16[64,192,128]{2,1,0:T(8,128)(2,1)}, u32[]{:S(2)}, u32[]{:S(2)}) collective-permute-start(bf16[64,192,128]{2,1,0:T(8,128)(2,1)S(1)} %copy.24.own), channel_id=1, source_target_pairs={{0,1},{1,0},{2,3},{3,2},{4,5},{5,4},{6,7},{7,6},{8,9},{9,8},{10,11... | collective-permute-start | bytes 9437192 | tf_op jit(solution)/shard_map/ppermute | solution.py:256

commit v2 on v1

--- a/solution.py
+++ b/solution.py
@@ -9,7 +9,6 @@
 
 MESH = pl.DeviceIdType.MESH
 CHUNKS = 3
-GROUP = 4
 TOP = 32767.0
 
 
@@ -69,15 +68,15 @@
     return ((ladder + partner) / denominator).astype(jnp.bfloat16)
 
 
-def ladder_kernel(pairs, tiles, loops, own, other, weights, ladder, codes, scales, picked, sems):
-    k, h, s = pl.program_id(0), pl.program_id(1), pl.program_id(2)
-    steps, halves, eight = pl.num_programs(0), pl.num_programs(1), pl.num_programs(2)
+def ladder_kernel(pairs, tiles, own, other, weights, ladder, codes, scales, picked, sems):
+    k, h = pl.program_id(0), pl.program_id(1)
+    steps, halves = pl.num_programs(0), pl.num_programs(1)
     held = own.shape[0]
     rows, depth = own.shape[1], own.shape[2]
-    wide = ladder.shape[3]
+    slots, wide = weights.shape[1], ladder.shape[3]
     half = wide // 2
 
-    @pl.when((k == 0) & (h == 0) & (s == 0))
+    @pl.when((k == 0) & (h == 0))
     def _():
         first = pltpu.make_async_copy(own, picked.at[pl.ds(0, held)], sems.at[0])
         second = pltpu.make_async_copy(other, picked.at[pl.ds(held, held)], sems.at[1])
@@ -87,17 +86,14 @@
         first.wait()
         second.wait()
 
-    a = (h * steps + k) * eight + s
-
-    def add(g, total):
-        lhs = jnp.concatenate([picked[tiles[a, g * GROUP + x]] for x in range(GROUP)], axis=1)
-        rhs = weights[0, pl.ds(g * GROUP, GROUP)].reshape(GROUP * depth, wide)
-        return total + jnp.dot(lhs, rhs, preferred_element_type=jnp.float32)
-
-    total = lax.fori_loop(0, loops[a], add, jnp.zeros((rows, wide), jnp.float32))
-    ladder[h, 0, pl.ds(s, rows, stride=8), :] = total
-
-    @pl.when((h == halves - 1) & (s == eight - 1))
+    for s in range(8):
+        a = (h * steps + k) * 8 + s
+        lhs = jnp.concatenate([picked[tiles[a, x]] for x in range(slots)], axis=1)
+        ladder[h, 0, pl.ds(s, rows, stride=8), :] = jnp.dot(
+            lhs, weights[s].reshape(slots * depth, wide), preferred_element_type=jnp.float32
+        )
+
+    @pl.when(h == halves - 1)
     def _():
         tall = codes.shape[3]
         low = lax.broadcasted_iota(jnp.int32, (tall, wide), 1) < half
@@ -232,7 +228,7 @@
     pairs, virts = lax.axis_size("pair"), lax.axis_size("virt")
     rows, others, held, depth = amplitudes.shape
     slots, wide = integrals.shape[1], integrals.shape[3]
-    fits = virts == 2 and held % 16 == 0 and rows % CHUNKS == 0 and slots % GROUP == 0
+    fits = virts == 2 and held % 16 == 0 and rows % CHUNKS == 0
     fits = fits and wide == 2 * held and wide == 128 and (rows // CHUNKS * rows) % 2 == 0
     if not fits:
         return general_device(amplitudes, integrals, cd_tiles, tile_counts, eps_occ, eps_virt)
@@ -246,7 +242,6 @@
     slot_ids = lax.broadcasted_iota(jnp.int32, cd_tiles.shape, 1)
     places = lax.rem(cd_tiles - first_tile + 2 * held, 2 * held)
     tiles = jnp.where(slot_ids < tile_counts[:, None], places, 2 * held)
-    loops = (tile_counts + GROUP - 1) // GROUP
 
     ladders, arrived, sizes = [], [], []
     swapped = []
@@ -259,20 +254,20 @@
         ladder, codes, scale = pl.pallas_call(
             functools.partial(ladder_kernel, pairs),
             grid_spec=pltpu.PrefetchScalarGridSpec(
-                num_scalar_prefetch=2,
-                grid=(steps, 2, 8),
+                num_scalar_prefetch=1,
+                grid=(steps, 2),
                 in_specs=[
                     pl.BlockSpec(memory_space=pl.ANY),
                     pl.BlockSpec(memory_space=pl.ANY),
                     pl.BlockSpec(
-                        (1, slots, depth, wide),
-                        lambda k, h, s, *_: ((h * steps + k) * 8 + s, 0, 0, 0),
+                        (8, slots, depth, wide),
+                        lambda k, h, *_: (h * steps + k, 0, 0, 0),
                     ),
                 ],
                 out_specs=[
-                    pl.BlockSpec((2, 1, count * 8, wide), lambda k, h, s, *_: (0, k, 0, 0)),
-                    pl.BlockSpec((pairs, 2, 1, tall, wide), lambda k, h, s, *_: (0, 0, k, 0, 0)),
-                    pl.BlockSpec((2, 8, wide), lambda k, h, s, *_: (0, 0, 0)),
+                    pl.BlockSpec((2, 1, count * 8, wide), lambda k, h, *_: (0, k, 0, 0)),
+                    pl.BlockSpec((pairs, 2, 1, tall, wide), lambda k, h, *_: (0, 0, k, 0, 0)),
+                    pl.BlockSpec((2, 8, wide), lambda k, h, *_: (0, 0, 0)),
                 ],
                 scratch_shapes=[
                     pltpu.VMEM((2 * held + 1, count, depth), amplitudes.dtype),
@@ -291,7 +286,7 @@
             ),
             compiler_params=pltpu.CompilerParams(vmem_limit_bytes=60 * 2**20),
             name=f"ladder_{r}",
-        )(tiles, loops, own, other, integrals)
+        )(tiles, own, other, integrals)
         got, size = pl.pallas_call(
             functools.partial(exchange_kernel, pairs, virts),
             in_specs=[pl.BlockSpec(memory_space=pl.ANY)] * 2,

time: 606 us -> 517 us (0.85)
  Pallas kernels: 523 us -> 436 us
    pallas_call x3, Pallas kernels: 241 us -> 111 us  [per_device(): pl.pallas_call(functools.partial(ladder_kernel, pairs), grid_spec=pltpu.P...]
    pallas_call x3, Pallas kernels: 252 us -> 295 us  [per_device(): pl.pallas_call(functools.partial(exchange_kernel, pairs, virts), in_specs...]
  transfers between devices with their start and end apart: 3 -> 3, of which waited for: 1 -> 1; matrix products, arithmetic and copies ran while one was open for 2% -> 2% of each run, Pallas kernels for 55% -> 56%
where the time goes in v2:
time: 517 us; the launch traced here: 516 us
  Pallas kernels  436 us (84%)
  waiting for transfers between devices  58.6 us (11%)
  local copies, waits for them, and re-layouts  18.7 us (4%)
    pallas_call x3, Pallas kernels, per_device(): pl.pallas_call(functools.partial(exchange_kernel, pairs, virts), in_specs...  295 us
    pallas_call x3, Pallas kernels, per_device(): pl.pallas_call(functools.partial(ladder_kernel, pairs), grid_spec=pltpu.P...  111 us
    ppermute x3, waiting for transfers between devices, per_device(): swapped.append((own, lax.ppermute(own, 'virt', [(0, 1), (1, 0)])))  58.6 us
    pallas_call x1, Pallas kernels, per_device(): pl.pallas_call(functools.partial(combine_kernel, CHUNKS, rows), grid=(pai...  29.3 us
  transfers between devices with their start and end apart: 3, of which 1 were waited for; matrix products, arithmetic and copies ran while one was open for 2% of the time, Pallas kernels for 56%

profile of v2, /device:TPU:15, one launch (start us, length us, event | category | flops | bytes accessed | tf_op | source)
XLA Modules:
  0.0 516.2 jit_solution(1566692395806439685)
XLA Ops:
  0.0 4.8 fusion.2
  4.9 0.7 copy.25
  5.6 3.7 copy.27.own
  9.3 0.2 collective-permute-start.2
  9.5 0.7 copy.19
  10.2 3.7 copy.21.own
  13.9 1.2 collective-permute-start
  15.1 0.7 copy.22
  15.8 0.0 copy-start.1
  15.8 0.0 copy-start.4
  15.9 0.0 copy-start.3
  15.9 0.0 copy-start.2
  15.9 2.0 copy.24.own
  17.9 0.0 copy-start
  17.9 0.3 collective-permute-start.1
  18.2 0.0 copy-done.1
  18.2 0.1 copy.18
  18.3 0.0 copy-done.4
  18.3 0.9 dynamic_slice.6.refs_0_
  19.2 0.0 copy-done.3
  19.2 0.1 dynamic_slice.7
  19.3 0.0 copy-done.2
  19.3 0.7 fusion.1.tiles
  20.0 58.6 %collective-permute-done.2.other = bf16[64,192,128]{2,1,0:T(8,128)(2,1)} collective-permute-done((bf16[64,192,128]{2,1,0:T(8,128)(2,1)}, bf16[64,192,128]{2,1,0:T(8,128)(2,1)}, u32[]{:S(2)}, u32[]{:S(2)}) %collective-permute-start.2) | collective-permute-done | bytes 3145760 | tf_op jit(solution)/shard_map/ppermute | solution.py:251
  78.6 37.2 %ladder_2.1 = (f32[2,4,1536,128]{3,2,1,0:T(8,128)}, s16[16,2,4,96,128]{4,3,2,1,0:T(8,128)(2,1)}, f32[2,8,128]{2,1,0:T(8,128)}) custom-call(s32[64,20]{1,0:T(8,128)} %fusion.1.tiles, bf16[64,192,128]{2,1,0:T(8,128)(2,1)} %copy.27.own, bf16[64,192,128]{2,1,0:T(8,128)(2,1)} %collective-permute-done.2.other, bf16[64,20,128,128]{3,2,1,0:T(8,128)(2,1)} %weights.5), custom_call_target="tpu_custom_call" | custom-call | flops 8053063680 | bytes 41943040 | tf_op jit(solution)/shard_map/ladder_2/pallas_call | solution.py:254
  115.8 0.0 copy-done
  115.8 134.9 %exchange_2.1 = (s16[16,2,4,96,128]{4,3,2,1,0:T(8,128)(2,1)}, f32[16,2,8,128]{3,2,1,0:T(8,128)}) custom-call(s16[16,2,4,96,128]{4,3,2,1,0:T(8,128)(2,1)} %get-tuple-element.29.codes, f32[2,8,128]{2,1,0:T(8,128)} %get-tuple-element.30.scales), custom_call_target="tpu_custom_call" | custom-call | tf_op jit(solution)/shard_map/exchange_2/pallas_call | solution.py:290
  250.8 0.0 collective-permute-done.other
  250.8 37.1 %ladder_0.1 = (f32[2,4,1536,128]{3,2,1,0:T(8,128)}, s16[16,2,4,96,128]{4,3,2,1,0:T(8,128)(2,1)}, f32[2,8,128]{2,1,0:T(8,128)}) custom-call(s32[64,20]{1,0:T(8,128)} %fusion.1.tiles, bf16[64,192,128]{2,1,0:T(8,128)(2,1)} %copy.21.own, bf16[64,192,128]{2,1,0:T(8,128)(2,1)} %collective-permute-done.other, bf16[64,20,128,128]{3,2,1,0:T(8,128)(2,1)} %weights.5), custom_call_target="tpu_custom_call" | custom-call | flops 8053063680 | bytes 41943040 | tf_op jit(solution)/shard_map/ladder_0/pallas_call | solution.py:254
  287.9 80.9 %exchange_0.1 = (s16[16,2,4,96,128]{4,3,2,1,0:T(8,128)(2,1)}, f32[16,2,8,128]{3,2,1,0:T(8,128)}) custom-call(s16[16,2,4,96,128]{4,3,2,1,0:T(8,128)(2,1)} %get-tuple-element.23.codes, f32[2,8,128]{2,1,0:T(8,128)} %get-tuple-element.24.scales), custom_call_target="tpu_custom_call" | custom-call | tf_op jit(solution)/shard_map/exchange_0/pallas_call | solution.py:290
  368.8 0.0 collective-permute-done.1.other
  368.8 37.1 %ladder_1.1 = (f32[2,4,1536,128]{3,2,1,0:T(8,128)}, s16[16,2,4,96,128]{4,3,2,1,0:T(8,128)(2,1)}, f32[2,8,128]{2,1,0:T(8,128)}) custom-call(s32[64,20]{1,0:T(8,128)} %fusion.1.tiles, bf16[64,192,128]{2,1,0:T(8,128)(2,1)} %copy-done, bf16[64,192,128]{2,1,0:T(8,128)(2,1)} %collective-permute-done.1.other, bf16[64,20,128,128]{3,2,1,0:T(8,128)(2,1)} %weights.5), custom_call_target="tpu_custom_call" | custom-call | flops 8053063680 | bytes 41943040 | tf_op jit(solution)/shard_map/ladder_1/pallas_call | solution.py:254
  405.8 79.7 %exchange_1.1 = (s16[16,2,4,96,128]{4,3,2,1,0:T(8,128)(2,1)}, f32[16,2,8,128]{3,2,1,0:T(8,128)}) custom-call(s16[16,2,4,96,128]{4,3,2,1,0:T(8,128)(2,1)} %get-tuple-element.26.codes, f32[2,8,128]{2,1,0:T(8,128)} %get-tuple-element.27.scales), custom_call_target="tpu_custom_call" | custom-call | tf_op jit(solution)/shard_map/exchange_1/pallas_call | solution.py:290
  485.5 0.7 broadcast_in_dim.6.refs_2_
  486.2 0.6 broadcast_in_dim.7.refs_3_
  486.8 29.3 %combine.1 = bf16[6,96,64,128]{3,2,1,0:T(8,128)(2,1)} custom-call(f32[6]{0:T(128)} %dynamic_slice.6.refs_0_, f32[96]{0:T(128)} %refs_1_.1, f32[64,128]{1,0:T(8,128)} %broadcast_in_dim.6.refs_2_, f32[64,128]{1,0:T(8,128)} %broadcast_in_dim.7.refs_3_, f32[2,4,16,96,128]{4,3,2,1,0:T(8,128)} %bitcast.22, f32[2,4,16,96,128]{4,3,2,1,0:T(8,128)} %bitcast.23, ...), custom_call_target="tpu_custom_call" | custom-call | tf_op jit(solution)/shard_map/combine/pallas_call | solution.py:310
Async XLA Ops:
  9.3 69.3 %collective-permute-start.2 = (bf16[64,192,128]{2,1,0:T(8,128)(2,1)}, bf16[64,192,128]{2,1,0:T(8,128)(2,1)}, u32[]{:S(2)}, u32[]{:S(2)}) collective-permute-start(bf16[64,192,128]{2,1,0:T(8,128)(2,1)} %copy.27.own), channel_id=1, source_target_pairs={{0,1},{1,0},{2,3},{3,2},{4,5},{5,4},{6,7},{7,6},{8,9},{9,8},{10,11... | collective-permute-start | bytes 9437192 | tf_op jit(solution)/shard_map/ppermute | solution.py:251
  13.9 236.9 %collective-permute-start = (bf16[64,192,128]{2,1,0:T(8,128)(2,1)}, bf16[64,192,128]{2,1,0:T(8,128)(2,1)}, u32[]{:S(2)}, u32[]{:S(2)}) collective-permute-start(bf16[64,192,128]{2,1,0:T(8,128)(2,1)} %copy.21.own), channel_id=1, source_target_pairs={{0,1},{1,0},{2,3},{3,2},{4,5},{5,4},{6,7},{7,6},{8,9},{9,8},{10,11... | collective-permute-start | bytes 9437192 | tf_op jit(solution)/shard_map/ppermute | solution.py:251
  15.8 2.4 copy-start.1
  15.8 2.5 copy-start.4
  15.9 3.3 copy-start.3
  15.9 3.4 copy-start.2
  17.9 97.9 %copy-start = (bf16[64,192,128]{2,1,0:T(8,128)(2,1)}, bf16[64,192,128]{2,1,0:T(8,128)(2,1)S(1)}, u32[]{:S(2)}) copy-start(bf16[64,192,128]{2,1,0:T(8,128)(2,1)S(1)} %copy.24.own) | copy-start | bytes 9437188
  17.9 350.8 %collective-permute-start.1 = (bf16[64,192,128]{2,1,0:T(8,128)(2,1)S(1)}, bf16[64,192,128]{2,1,0:T(8,128)(2,1)}, u32[]{:S(2)}, u32[]{:S(2)}) collective-permute-start(bf16[64,192,128]{2,1,0:T(8,128)(2,1)S(1)} %copy.24.own), channel_id=1, source_target_pairs={{0,1},{1,0},{2,3},{3,2},{4,5},{5,4},{6,7},{7,6},{8,9},{9,8},{10,11... | collective-permute-start | bytes 9437192 | tf_op jit(solution)/shard_map/ppermute | solution.py:251

commit v3 on v2

--- a/solution.py
+++ b/solution.py
@@ -8,7 +8,7 @@
 from jax.sharding import PartitionSpec as P
 
 MESH = pl.DeviceIdType.MESH
-CHUNKS = 3
+CHUNKS = 6
 TOP = 32767.0
 
 
@@ -128,34 +128,29 @@
         lax.fori_loop(0, pairs, pack, 0)
 
 
-def exchange_kernel(pairs, virts, codes, scales, arrived, sizes, send, recv, send_s, recv_s, own):
-    mine_p, mine_v = lax.axis_index("pair"), lax.axis_index("virt")
-    me = mine_p * virts + mine_v
-    count = pairs * virts
-    barrier = pltpu.get_barrier_semaphore()
-
-    def target(d):
-        t = lax.rem(me + d, count)
-        return t // virts, lax.rem(t, virts)
-
-    def greet(d, _):
-        p, v = target(d)
-        pl.semaphore_signal(barrier, inc=1, device_id=(p, v), device_id_type=MESH)
-        return 0
-
-    lax.fori_loop(1, count, greet, 0)
-    keep = pltpu.make_async_copy(codes.at[mine_p, mine_v], arrived.at[mine_p, mine_v], own.at[0])
-    keep_s = pltpu.make_async_copy(scales.at[mine_v], sizes.at[mine_p, mine_v], own.at[1])
-    keep.start()
-    keep_s.start()
-    pl.semaphore_wait(barrier, count - 1)
-
-    def copies(d):
-        p, v = target(d)
+class Exchange:
+    def __init__(self, pairs, virts, codes, scales, arrived, sizes, send, recv, send_s, recv_s, own):
+        self.refs = codes, scales, arrived, sizes, send, recv, send_s, recv_s
+        self.virts, self.count = virts, pairs * virts
+        self.here = lax.axis_index("pair"), lax.axis_index("virt")
+        p, v = self.here
+        self.me = p * virts + v
+        self.kept = (
+            pltpu.make_async_copy(codes.at[p, v], arrived.at[p, v], own.at[0]),
+            pltpu.make_async_copy(scales.at[v], sizes.at[p, v], own.at[1]),
+        )
+
+    def target(self, d):
+        t = lax.rem(self.me + d, self.count)
+        return t // self.virts, lax.rem(t, self.virts)
+
+    def copies(self, d):
+        codes, scales, arrived, sizes, send, recv, send_s, recv_s = self.refs
+        p, v = self.target(d)
         return (
             pltpu.make_async_remote_copy(
                 src_ref=codes.at[p, v],
-                dst_ref=arrived.at[mine_p, mine_v],
+                dst_ref=arrived.at[self.here],
                 send_sem=send.at[d],
                 recv_sem=recv.at[d],
                 device_id=(p, v),
@@ -163,7 +158,7 @@
             ),
             pltpu.make_async_remote_copy(
                 src_ref=scales.at[v],
-                dst_ref=sizes.at[mine_p, mine_v],
+                dst_ref=sizes.at[self.here],
                 send_sem=send_s.at[d],
                 recv_sem=recv_s.at[d],
                 device_id=(p, v),
@@ -171,20 +166,55 @@
             ),
         )
 
-    def begin(d, _):
-        for copy in copies(d):
+    def start(self):
+        barrier = pltpu.get_barrier_semaphore()
+
+        def greet(d, _):
+            pl.semaphore_signal(barrier, inc=1, device_id=self.target(d), device_id_type=MESH)
+            return 0
+
+        def begin(d, _):
+            for copy in self.copies(d):
+                copy.start()
+            return 0
+
+        lax.fori_loop(1, self.count, greet, 0)
+        pl.semaphore_wait(barrier, self.count - 1)
+        lax.fori_loop(1, self.count, begin, 0)
+        for copy in self.kept:
             copy.start()
-        return 0
-
-    def finish(d, _):
-        for copy in copies(d):
+
+    def wait(self):
+        def finish(d, _):
+            for copy in self.copies(d):
+                copy.wait()
+            return 0
+
+        lax.fori_loop(1, self.count, finish, 0)
+        for copy in self.kept:
             copy.wait()
-        return 0
-
-    lax.fori_loop(1, count, begin, 0)
-    lax.fori_loop(1, count, finish, 0)
-    keep.wait()
-    keep_s.wait()
+
+
+def exchange_kernel(pairs, virts, *refs):
+    moved = Exchange(pairs, virts, *refs)
+    moved.start()
+    moved.wait()
+
+
+def both_kernel(pairs, virts, tiles, own, other, weights, old_codes, old_scales, *refs):
+    ladder, codes, scales, arrived, sizes, picked, sems = refs[:7]
+    moved = Exchange(pairs, virts, old_codes, old_scales, arrived, sizes, *refs[7:])
+    k, h = pl.program_id(0), pl.program_id(1)
+
+    @pl.when((k == 0) & (h == 0))
+    def _():
+        moved.start()
+
+    ladder_kernel(pairs, tiles, own, other, weights, ladder, codes, scales, picked, sems)
+
+    @pl.when((k == pl.num_programs(0) - 1) & (h == pl.num_programs(1) - 1))
+    def _():
+        moved.wait()
 
 
 def combine_kernel(chunks, rows, *refs):
@@ -249,60 +279,73 @@
         own = amplitudes[r * part : (r + 1) * part].reshape(part, pairs, rows, held, depth)
         own = jnp.transpose(own, (3, 1, 0, 2, 4)).reshape(held, count, depth)
         swapped.append((own, lax.ppermute(own, "virt", [(0, 1), (1, 0)])))
+    anywhere = pl.BlockSpec(memory_space=pl.ANY)
+    moved_sems = [pltpu.SemaphoreType.DMA((pairs * virts,))] * 4 + [pltpu.SemaphoreType.DMA((2,))]
+    moved_shape = [
+        jax.ShapeDtypeStruct((pairs, 2, steps, tall, wide), jnp.int16),
+        jax.ShapeDtypeStruct((pairs, 2, 8, wide), jnp.float32),
+    ]
+    last = ()
     for r in range(CHUNKS):
         own, other = swapped[r]
-        ladder, codes, scale = pl.pallas_call(
-            functools.partial(ladder_kernel, pairs),
+        beside = len(last) > 0
+        kernel = functools.partial(both_kernel, pairs, virts)
+        extra = {"collective_id": r, "has_side_effects": True} if beside else {}
+        ladder, *made = pl.pallas_call(
+            kernel if beside else functools.partial(ladder_kernel, pairs),
             grid_spec=pltpu.PrefetchScalarGridSpec(
                 num_scalar_prefetch=1,
                 grid=(steps, 2),
                 in_specs=[
-                    pl.BlockSpec(memory_space=pl.ANY),
-                    pl.BlockSpec(memory_space=pl.ANY),
+                    anywhere,
+                    anywhere,
                     pl.BlockSpec(
-                        (8, slots, depth, wide),
-                        lambda k, h, *_: (h * steps + k, 0, 0, 0),
+                        (8, slots, depth, wide), lambda k, h, *_: (h * steps + k, 0, 0, 0)
                     ),
-                ],
+                ]
+                + [anywhere] * len(last),
                 out_specs=[
                     pl.BlockSpec((2, 1, count * 8, wide), lambda k, h, *_: (0, k, 0, 0)),
                     pl.BlockSpec((pairs, 2, 1, tall, wide), lambda k, h, *_: (0, 0, k, 0, 0)),
                     pl.BlockSpec((2, 8, wide), lambda k, h, *_: (0, 0, 0)),
-                ],
+                ]
+                + [anywhere] * len(last),
                 scratch_shapes=[
                     pltpu.VMEM((2 * held + 1, count, depth), amplitudes.dtype),
                     pltpu.SemaphoreType.DMA((2,)),
-                ],
+                ]
+                + moved_sems * beside,
             ),
             out_shape=[
                 jax.ShapeDtypeStruct((2, steps, count * 8, wide), jnp.float32),
                 jax.ShapeDtypeStruct((pairs, 2, steps, tall, wide), jnp.int16),
                 jax.ShapeDtypeStruct((2, 8, wide), jnp.float32),
-            ],
+            ]
+            + moved_shape * beside,
             cost_estimate=pl.CostEstimate(
                 flops=2 * count * held * slots * depth * wide,
                 bytes_accessed=2 * integrals.size,
                 transcendentals=0,
             ),
-            compiler_params=pltpu.CompilerParams(vmem_limit_bytes=60 * 2**20),
+            compiler_params=pltpu.CompilerParams(vmem_limit_bytes=60 * 2**20, **extra),
             name=f"ladder_{r}",
-        )(tiles, own, other, integrals)
-        got, size = pl.pallas_call(
-            functools.partial(exchange_kernel, pairs, virts),
-            in_specs=[pl.BlockSpec(memory_space=pl.ANY)] * 2,
-            out_specs=[pl.BlockSpec(memory_space=pl.ANY)] * 2,
-            out_shape=[
-                jax.ShapeDtypeStruct(codes.shape, codes.dtype),
-                jax.ShapeDtypeStruct((pairs,) + scale.shape, scale.dtype),
-            ],
-            scratch_shapes=[pltpu.SemaphoreType.DMA((pairs * virts,))] * 4
-            + [pltpu.SemaphoreType.DMA((2,))],
-            compiler_params=pltpu.CompilerParams(collective_id=r, has_side_effects=True),
-            name=f"exchange_{r}",
-        )(codes, scale)
+        )(tiles, own, other, integrals, *last)
+        last = tuple(made[:2])
         ladders.append(ladder.reshape(2, steps, pairs, tall, wide))
-        arrived.append(got)
-        sizes.append(size)
+        if beside:
+            arrived.append(made[2])
+            sizes.append(made[3])
+    got, size = pl.pallas_call(
+        functools.partial(exchange_kernel, pairs, virts),
+        in_specs=[anywhere] * 2,
+        out_specs=[anywhere] * 2,
+        out_shape=moved_shape,
+        scratch_shapes=moved_sems,
+        compiler_params=pltpu.CompilerParams(collective_id=CHUNKS, has_side_effects=True),
+        name="exchange",
+    )(*last)
+    arrived.append(got)
+    sizes.append(size)
     occ_own = lax.dynamic_slice_in_dim(eps_occ, first_row, rows)
     virt_own = lax.dynamic_slice_in_dim(eps_virt, first_tile, held)
     smem = pl.BlockSpec(memory_space=pltpu.SMEM)

time: 517 us -> 504 us (0.975)
  waiting for transfers between devices: 58.6 us -> 24.9 us
  Pallas kernels: 436 us -> 453 us
    pallas_call x3 -> x6, Pallas kernels: 111 us -> 379 us  [per_device(): pl.pallas_call(kernel if beside else functools.partial(ladder_kernel, pai...]
    pallas_call x3 -> x1, Pallas kernels: 295 us -> 43.7 us  [per_device(): pl.pallas_call(functools.partial(exchange_kernel, pairs, virts), in_specs...]
    ppermute x3 -> x6, waiting for transfers between devices: 58.6 us -> 24.9 us  [per_device(): swapped.append((own, lax.ppermute(own, 'virt', [(0, 1), (1, 0)])))]
    reshape x3 -> x7, local copies, waits for them, and re-layouts: 9.46 us -> 17.8 us  [per_device(): own = jnp.transpose(own, (3, 1, 0, 2, 4)).reshape(held, count, depth)]
  transfers between devices with their start and end apart: 3 -> 6, of which waited for: 1 -> 2; matrix products, arithmetic and copies ran while one was open for 2% -> 2% of each run, Pallas kernels for 56% -> 66%
where the time goes in v3:
time: 504 us; the launch traced here: 502 us
  Pallas kernels  453 us (90%)
  waiting for transfers between devices  24.9 us (5%)
  local copies, waits for them, and re-layouts  19.9 us (4%)
    pallas_call x6, Pallas kernels, per_device(): pl.pallas_call(kernel if beside else functools.partial(ladder_kernel, pai...  379 us
    pallas_call x1, Pallas kernels, per_device(): pl.pallas_call(functools.partial(exchange_kernel, pairs, virts), in_specs...  43.7 us
    pallas_call x1, Pallas kernels, per_device(): pl.pallas_call(functools.partial(combine_kernel, CHUNKS, rows), grid=(pai...  30.1 us
    ppermute x6, waiting for transfers between devices, per_device(): swapped.append((own, lax.ppermute(own, 'virt', [(0, 1), (1, 0)])))  24.9 us
    reshape x7, local copies, waits for them, and re-layouts, per_device(): own = jnp.transpose(own, (3, 1, 0, 2, 4)).reshape(held, count, depth)  17.8 us
  transfers between devices with their start and end apart: 6, of which 2 were waited for; matrix products, arithmetic and copies ran while one was open for 2% of the time, Pallas kernels for 66%

profile of v3, /device:TPU:15, one launch (start us, length us, event | category | flops | bytes accessed | tf_op | source)
XLA Modules:
  0.0 502.1 jit_solution(3851068277833563384)
XLA Ops:
  0.0 5.7 %slice_bitcast_fusion = (bf16[64,96,128]{2,0,1:T(8,128)(2,1)}, bf16[64,96,128]{2,0,1:T(8,128)(2,1)S(1)}, bf16[64,96,128]{2,0,1:T(8,128)(2,1)S(1)}, bf16[64,96,12...) fusion(bf16[6,96,64,128]{3,2,1,0:T(8,128)(2,1)} %param.6), kind=kLoop, calls=%fused_computation | loop fusion | bytes 18874368 | tf_op jit(solution)/shard_map/reshape | solution.py:280
  5.7 2.2 copy.16.own
  7.9 0.2 collective-permute-start
  8.1 2.2 copy.18.own
  10.2 1.2 collective-permute-start.1
  11.5 2.2 copy.20.own
  13.6 0.2 collective-permute-start.2
  13.9 1.0 copy.22.own
  14.9 0.0 copy-start.1
  14.9 1.3 collective-permute-start.3
  16.2 0.0 copy-start.2
  16.2 0.0 copy-start.3
  16.2 1.0 copy.24.own
  17.2 0.0 copy-done.1
  17.2 0.0 copy-start
  17.2 0.3 collective-permute-start.4
  17.5 0.0 copy-done.2
  17.5 0.1 copy.14
  17.6 0.0 copy-done.3
  17.6 0.8 fusion.1.tiles
  18.4 0.0 copy-start.5
  18.4 0.0 copy-start.4
  18.4 3.6 copy.26.own
  22.0 0.0 copy-done
  22.0 0.0 copy-done.5
  22.0 0.7 dynamic_slice.6.refs_0_
  22.7 0.0 copy-done.4
  22.7 0.1 dynamic_slice.7
  22.7 20.7 %collective-permute-done.other = bf16[64,96,128]{2,1,0:T(8,128)(2,1)} collective-permute-done((bf16[64,96,128]{2,1,0:T(8,128)(2,1)}, bf16[64,96,128]{2,1,0:T(8,128)(2,1)}, u32[]{:S(2)}, u32[]{:S(2)}) %collective-permute-start) | collective-permute-done | bytes 1572896 | tf_op jit(solution)/shard_map/ppermute | solution.py:281
  43.5 0.2 collective-permute-start.5
  43.7 29.3 %ladder_0.1 = (f32[2,4,768,128]{3,2,1,0:T(8,128)}, s16[16,2,4,48,128]{4,3,2,1,0:T(8,128)(2,1)}, f32[2,8,128]{2,1,0:T(8,128)}) custom-call(s32[64,20]{1,0:T(8,128)} %fusion.1.tiles, bf16[64,96,128]{2,1,0:T(8,128)(2,1)} %copy.16.own, bf16[64,96,128]{2,1,0:T(8,128)(2,1)} %collective-permute-done.other, bf16[64,20,128,128]{3,2,1,0:T(8,128)(2,1)} %weights.11), custom_call_target="tpu_custom_call" | custom-call | flops 4026531840 | bytes 41943040 | tf_op jit(solution)/shard_map/ladder_0/pallas_call | solution.py:294
  73.0 4.2 collective-permute-done.1.other
  77.2 156.4 %ladder_1.1 = (f32[2,4,768,128]{3,2,1,0:T(8,128)}, s16[16,2,4,48,128]{4,3,2,1,0:T(8,128)(2,1)}, f32[2,8,128]{2,1,0:T(8,128)}, s16[16,2,4,48,128]{4,3,2,1,0:T(8,128)(2,1)}, f32[16,2,8,128]{3,2,1,0:T(8,128)}) custom-call(s32[64,20]{1,0:T(8,128)} %fusion.1.tiles, bf16[64,96,128]{2,1,0:T(8,128)(2,1)} %copy.18.own, ...), custom_call_target="tpu_custom_call" | custom-call | flops 4026531840 | bytes 41943040 | tf_op jit(solution)/shard_map/ladder_1/pallas_call | solution.py:294
  233.6 0.0 collective-permute-done.2.other
  233.6 48.9 %ladder_2.1 = (f32[2,4,768,128]{3,2,1,0:T(8,128)}, s16[16,2,4,48,128]{4,3,2,1,0:T(8,128)(2,1)}, f32[2,8,128]{2,1,0:T(8,128)}, s16[16,2,4,48,128]{4,3,2,1,0:T(8,128)(2,1)}, f32[16,2,8,128]{3,2,1,0:T(8,128)}) custom-call(s32[64,20]{1,0:T(8,128)} %fusion.1.tiles, bf16[64,96,128]{2,1,0:T(8,128)(2,1)} %copy.20.own, ...), custom_call_target="tpu_custom_call" | custom-call | flops 4026531840 | bytes 41943040 | tf_op jit(solution)/shard_map/ladder_2/pallas_call | solution.py:294
  282.5 0.0 collective-permute-done.3.other
  282.5 48.1 %ladder_3.1 = (f32[2,4,768,128]{3,2,1,0:T(8,128)}, s16[16,2,4,48,128]{4,3,2,1,0:T(8,128)(2,1)}, f32[2,8,128]{2,1,0:T(8,128)}, s16[16,2,4,48,128]{4,3,2,1,0:T(8,128)(2,1)}, f32[16,2,8,128]{3,2,1,0:T(8,128)}) custom-call(s32[64,20]{1,0:T(8,128)} %fusion.1.tiles, bf16[64,96,128]{2,1,0:T(8,128)(2,1)} %copy-done.1, ...), custom_call_target="tpu_custom_call" | custom-call | flops 4026531840 | bytes 41943040 | tf_op jit(solution)/shard_map/ladder_3/pallas_call | solution.py:294
  330.5 0.0 collective-permute-done.4.other
  330.6 48.1 %ladder_4.1 = (f32[2,4,768,128]{3,2,1,0:T(8,128)}, s16[16,2,4,48,128]{4,3,2,1,0:T(8,128)(2,1)}, f32[2,8,128]{2,1,0:T(8,128)}, s16[16,2,4,48,128]{4,3,2,1,0:T(8,128)(2,1)}, f32[16,2,8,128]{3,2,1,0:T(8,128)}) custom-call(s32[64,20]{1,0:T(8,128)} %fusion.1.tiles, bf16[64,96,128]{2,1,0:T(8,128)(2,1)} %copy-done, ...), custom_call_target="tpu_custom_call" | custom-call | flops 4026531840 | bytes 41943040 | tf_op jit(solution)/shard_map/ladder_4/pallas_call | solution.py:294
  378.7 0.0 collective-permute-done.5.other
  378.7 48.1 %ladder_5.1 = (f32[2,4,768,128]{3,2,1,0:T(8,128)}, s16[16,2,4,48,128]{4,3,2,1,0:T(8,128)(2,1)}, f32[2,8,128]{2,1,0:T(8,128)}, s16[16,2,4,48,128]{4,3,2,1,0:T(8,128)(2,1)}, f32[16,2,8,128]{3,2,1,0:T(8,128)}) custom-call(s32[64,20]{1,0:T(8,128)} %fusion.1.tiles, bf16[64,96,128]{2,1,0:T(8,128)(2,1)} %copy.26.own, ...), custom_call_target="tpu_custom_call" | custom-call | flops 4026531840 | bytes 41943040 | tf_op jit(solution)/shard_map/ladder_5/pallas_call | solution.py:294
  426.8 43.7 %exchange.1 = (s16[16,2,4,48,128]{4,3,2,1,0:T(8,128)(2,1)}, f32[16,2,8,128]{3,2,1,0:T(8,128)}) custom-call(s16[16,2,4,48,128]{4,3,2,1,0:T(8,128)(2,1)} %get-tuple-element.56.refs_0_, f32[2,8,128]{2,1,0:T(8,128)} %get-tuple-element.57.refs_1_), custom_call_target="tpu_custom_call" | custom-call | tf_op jit(solution)/shard_map/exchange/pallas_call | solution.py:338
  470.5 0.7 broadcast_in_dim.6.refs_2_
  471.2 0.6 broadcast_in_dim.7.refs_3_
  471.8 30.1 %combine.1 = bf16[6,96,64,128]{3,2,1,0:T(8,128)(2,1)} custom-call(f32[6]{0:T(128)} %dynamic_slice.6.refs_0_, f32[96]{0:T(128)} %refs_1_.1, f32[64,128]{1,0:T(8,128)} %broadcast_in_dim.6.refs_2_, f32[64,128]{1,0:T(8,128)} %broadcast_in_dim.7.refs_3_, f32[2,4,16,48,128]{4,3,2,1,0:T(8,128)} %bitcast.42, f32[2,4,16,48,128]{4,3,2,1,0:T(8,128)} %bitcast.43, ...), custom_call_target="tpu_custom_call" | custom-call | tf_op jit(solution)/shard_map/combine/pallas_call | solution.py:353
Async XLA Ops:
  7.9 35.6 %collective-permute-start = (bf16[64,96,128]{2,1,0:T(8,128)(2,1)}, bf16[64,96,128]{2,1,0:T(8,128)(2,1)}, u32[]{:S(2)}, u32[]{:S(2)}) collective-permute-start(bf16[64,96,128]{2,1,0:T(8,128)(2,1)} %copy.16.own), channel_id=1, source_target_pairs={{0,1},{1,0},{2,3},{3,2},{4,5},{5,4},{6,7},{7,6},{8,9},{9,8},{10,11... | collective-permute-start | bytes 4718600 | tf_op jit(solution)/shard_map/ppermute | solution.py:281
  10.2 66.9 %collective-permute-start.1 = (bf16[64,96,128]{2,1,0:T(8,128)(2,1)}, bf16[64,96,128]{2,1,0:T(8,128)(2,1)}, u32[]{:S(2)}, u32[]{:S(2)}) collective-permute-start(bf16[64,96,128]{2,1,0:T(8,128)(2,1)} %copy.18.own), channel_id=1, source_target_pairs={{0,1},{1,0},{2,3},{3,2},{4,5},{5,4},{6,7},{7,6},{8,9},{9,8},{10,11... | collective-permute-start | bytes 4718600 | tf_op jit(solution)/shard_map/ppermute | solution.py:281
  13.6 219.9 %collective-permute-start.2 = (bf16[64,96,128]{2,1,0:T(8,128)(2,1)}, bf16[64,96,128]{2,1,0:T(8,128)(2,1)}, u32[]{:S(2)}, u32[]{:S(2)}) collective-permute-start(bf16[64,96,128]{2,1,0:T(8,128)(2,1)} %copy.20.own), channel_id=1, source_target_pairs={{0,1},{1,0},{2,3},{3,2},{4,5},{5,4},{6,7},{7,6},{8,9},{9,8},{10,11... | collective-permute-start | bytes 4718600 | tf_op jit(solution)/shard_map/ppermute | solution.py:281
  14.9 2.3 copy-start.1
  14.9 267.6 %collective-permute-start.3 = (bf16[64,96,128]{2,1,0:T(8,128)(2,1)S(1)}, bf16[64,96,128]{2,1,0:T(8,128)(2,1)}, u32[]{:S(2)}, u32[]{:S(2)}) collective-permute-start(bf16[64,96,128]{2,1,0:T(8,128)(2,1)S(1)} %copy.22.own), channel_id=1, source_target_pairs={{0,1},{1,0},{2,3},{3,2},{4,5},{5,4},{6,7},{7,6},{8,9},{9,8},{10,11... | collective-permute-start | bytes 4718600 | tf_op jit(solution)/shard_map/ppermute | solution.py:281
  16.2 1.3 copy-start.2
  16.2 1.4 copy-start.3
  17.2 4.8 copy-start
  17.2 313.3 %collective-permute-start.4 = (bf16[64,96,128]{2,1,0:T(8,128)(2,1)S(1)}, bf16[64,96,128]{2,1,0:T(8,128)(2,1)}, u32[]{:S(2)}, u32[]{:S(2)}) collective-permute-start(bf16[64,96,128]{2,1,0:T(8,128)(2,1)S(1)} %copy.24.own), channel_id=1, source_target_pairs={{0,1},{1,0},{2,3},{3,2},{4,5},{5,4},{6,7},{7,6},{8,9},{9,8},{10,11... | collective-permute-start | bytes 4718600 | tf_op jit(solution)/shard_map/ppermute | solution.py:281
  18.4 3.6 copy-start.5
  18.4 4.3 copy-start.4
  43.5 335.2 %collective-permute-start.5 = (bf16[64,96,128]{2,1,0:T(8,128)(2,1)}, bf16[64,96,128]{2,1,0:T(8,128)(2,1)}, u32[]{:S(2)}, u32[]{:S(2)}) collective-permute-start(bf16[64,96,128]{2,1,0:T(8,128)(2,1)} %copy.26.own), channel_id=1, source_target_pairs={{0,1},{1,0},{2,3},{3,2},{4,5},{5,4},{6,7},{7,6},{8,9},{9,8},{10,11... | collective-permute-start | bytes 4718600 | tf_op jit(solution)/shard_map/ppermute | solution.py:281

commit v4 on v3

--- a/solution.py
+++ b/solution.py
@@ -167,19 +167,11 @@
         )
 
     def start(self):
-        barrier = pltpu.get_barrier_semaphore()
-
-        def greet(d, _):
-            pl.semaphore_signal(barrier, inc=1, device_id=self.target(d), device_id_type=MESH)
-            return 0
-
         def begin(d, _):
             for copy in self.copies(d):
                 copy.start()
             return 0
 
-        lax.fori_loop(1, self.count, greet, 0)
-        pl.semaphore_wait(barrier, self.count - 1)
         lax.fori_loop(1, self.count, begin, 0)
         for copy in self.kept:
             copy.start()
@@ -195,26 +187,66 @@
             copy.wait()
 
 
+def greet_all(pairs, virts):
+    count = pairs * virts
+    me = lax.axis_index("pair") * virts + lax.axis_index("virt")
+    barrier = pltpu.get_barrier_semaphore()
+
+    def greet(d, _):
+        t = lax.rem(me + d, count)
+        pl.semaphore_signal(
+            barrier, inc=1, device_id=(t // virts, lax.rem(t, virts)), device_id_type=MESH
+        )
+        return 0
+
+    lax.fori_loop(1, count, greet, 0)
+    pl.semaphore_wait(barrier, count - 1)
+
+
 def exchange_kernel(pairs, virts, *refs):
     moved = Exchange(pairs, virts, *refs)
+    greet_all(pairs, virts)
     moved.start()
     moved.wait()
 
 
-def both_kernel(pairs, virts, tiles, own, other, weights, old_codes, old_scales, *refs):
-    ladder, codes, scales, arrived, sizes, picked, sems = refs[:7]
-    moved = Exchange(pairs, virts, old_codes, old_scales, arrived, sizes, *refs[7:])
+def both_kernel(pairs, virts, beside, more, tiles, own, other, weights, *refs):
+    refs = list(refs)
+    old = [refs.pop(0) for _ in range(2 * beside)]
+    ahead = [refs.pop(0) for _ in range(more)]
+    ladder, codes, scales = [refs.pop(0) for _ in range(3)]
+    old += [refs.pop(0) for _ in range(2 * beside)]
+    ahead += [refs.pop(0) for _ in range(more)]
+    picked, sems = refs.pop(0), refs.pop(0)
+    tasks = []
+    if beside:
+        tasks.append(Exchange(pairs, virts, *old, *[refs.pop(0) for _ in range(5)]))
+    if more:
+        swap_sems = refs.pop(0)
+        tasks.append(
+            pltpu.make_async_remote_copy(
+                src_ref=ahead[0],
+                dst_ref=ahead[1],
+                send_sem=swap_sems.at[0],
+                recv_sem=swap_sems.at[1],
+                device_id=(lax.axis_index("pair"), 1 - lax.axis_index("virt")),
+                device_id_type=MESH,
+            )
+        )
     k, h = pl.program_id(0), pl.program_id(1)
 
     @pl.when((k == 0) & (h == 0))
     def _():
-        moved.start()
+        greet_all(pairs, virts)
+        for task in tasks:
+            task.start()
 
     ladder_kernel(pairs, tiles, own, other, weights, ladder, codes, scales, picked, sems)
 
     @pl.when((k == pl.num_programs(0) - 1) & (h == pl.num_programs(1) - 1))
     def _():
-        moved.wait()
+        for task in tasks:
+            task.wait()
 
 
 def combine_kernel(chunks, rows, *refs):
@@ -278,7 +310,8 @@
     for r in range(CHUNKS):
         own = amplitudes[r * part : (r + 1) * part].reshape(part, pairs, rows, held, depth)
         own = jnp.transpose(own, (3, 1, 0, 2, 4)).reshape(held, count, depth)
-        swapped.append((own, lax.ppermute(own, "virt", [(0, 1), (1, 0)])))
+        swapped.append(own)
+    other = lax.ppermute(swapped[0], "virt", [(0, 1), (1, 0)])
     anywhere = pl.BlockSpec(memory_space=pl.ANY)
     moved_sems = [pltpu.SemaphoreType.DMA((pairs * virts,))] * 4 + [pltpu.SemaphoreType.DMA((2,))]
     moved_shape = [
@@ -287,12 +320,12 @@
     ]
     last = ()
     for r in range(CHUNKS):
-        own, other = swapped[r]
+        own = swapped[r]
         beside = len(last) > 0
-        kernel = functools.partial(both_kernel, pairs, virts)
-        extra = {"collective_id": r, "has_side_effects": True} if beside else {}
+        ahead = swapped[r + 1 : r + 2]
+        more = len(ahead)
         ladder, *made = pl.pallas_call(
-            kernel if beside else functools.partial(ladder_kernel, pairs),
+            functools.partial(both_kernel, pairs, virts, beside, more),
             grid_spec=pltpu.PrefetchScalarGridSpec(
                 num_scalar_prefetch=1,
                 grid=(steps, 2),
@@ -303,38 +336,43 @@
                         (8, slots, depth, wide), lambda k, h, *_: (h * steps + k, 0, 0, 0)
                     ),
                 ]
-                + [anywhere] * len(last),
+                + [anywhere] * (len(last) + more),
                 out_specs=[
                     pl.BlockSpec((2, 1, count * 8, wide), lambda k, h, *_: (0, k, 0, 0)),
                     pl.BlockSpec((pairs, 2, 1, tall, wide), lambda k, h, *_: (0, 0, k, 0, 0)),
                     pl.BlockSpec((2, 8, wide), lambda k, h, *_: (0, 0, 0)),
                 ]
-                + [anywhere] * len(last),
+                + [anywhere] * (len(last) + more),
                 scratch_shapes=[
                     pltpu.VMEM((2 * held + 1, count, depth), amplitudes.dtype),
                     pltpu.SemaphoreType.DMA((2,)),
                 ]
-                + moved_sems * beside,
+                + moved_sems * beside
+                + [pltpu.SemaphoreType.DMA((2,))] * more,
             ),
             out_shape=[
                 jax.ShapeDtypeStruct((2, steps, count * 8, wide), jnp.float32),
                 jax.ShapeDtypeStruct((pairs, 2, steps, tall, wide), jnp.int16),
                 jax.ShapeDtypeStruct((2, 8, wide), jnp.float32),
             ]
-            + moved_shape * beside,
+            + moved_shape * beside
+            + [jax.ShapeDtypeStruct(own.shape, own.dtype)] * more,
             cost_estimate=pl.CostEstimate(
                 flops=2 * count * held * slots * depth * wide,
                 bytes_accessed=2 * integrals.size,
                 transcendentals=0,
             ),
-            compiler_params=pltpu.CompilerParams(vmem_limit_bytes=60 * 2**20, **extra),
+            compiler_params=pltpu.CompilerParams(
+                vmem_limit_bytes=60 * 2**20, collective_id=r, has_side_effects=True
+            ),
             name=f"ladder_{r}",
-        )(tiles, own, other, integrals, *last)
+        )(tiles, own, other, integrals, *last, *ahead)
         last = tuple(made[:2])
         ladders.append(ladder.reshape(2, steps, pairs, tall, wide))
         if beside:
             arrived.append(made[2])
             sizes.append(made[3])
+        other = made[-1]
     got, size = pl.pallas_call(
         functools.partial(exchange_kernel, pairs, virts),
         in_specs=[anywhere] * 2,

time: 504 us -> 466 us (0.925)
  Pallas kernels: 453 us -> 420 us
    pallas_call x6, Pallas kernels: 379 us -> 347 us  [per_device(): pl.pallas_call(functools.partial(both_kernel, pairs, virts, beside, more)...]
    ppermute x6 -> x1, waiting for transfers between devices: 24.9 us -> 21.2 us  [per_device(): other = lax.ppermute(swapped[0], 'virt', [(0, 1), (1, 0)])]
  transfers between devices with their start and end apart: 6 -> 1, of which waited for: 2 -> 1; matrix products, arithmetic and copies ran while one was open for 2% -> 3% of each run, Pallas kernels for 66% -> 0%
where the time goes in v4:
time: 466 us; the launch traced here: 464 us
  Pallas kernels  420 us (90%)
  local copies, waits for them, and re-layouts  22.1 us (5%)
  waiting for transfers between devices  21.2 us (5%)
    pallas_call x6, Pallas kernels, per_device(): pl.pallas_call(functools.partial(both_kernel, pairs, virts, beside, more)...  347 us
    pallas_call x1, Pallas kernels, per_device(): pl.pallas_call(functools.partial(exchange_kernel, pairs, virts), in_specs...  42.8 us
    pallas_call x1, Pallas kernels, per_device(): pl.pallas_call(functools.partial(combine_kernel, CHUNKS, rows), grid=(pai...  30.1 us
    ppermute x1, waiting for transfers between devices, per_device(): other = lax.ppermute(swapped[0], 'virt', [(0, 1), (1, 0)])  21.2 us
    reshape x7, local copies, waits for them, and re-layouts, per_device(): own = jnp.transpose(own, (3, 1, 0, 2, 4)).reshape(held, count, depth)  20 us
  transfers between devices with their start and end apart: 1, of which 1 were waited for; matrix products, arithmetic and copies ran while one was open for 3% of the time, Pallas kernels for 0%

profile of v4, /device:TPU:15, one launch (start us, length us, event | category | flops | bytes accessed | tf_op | source)
XLA Modules:
  0.0 464.2 jit_solution(5057370226176489138)
XLA Ops:
  0.0 6.5 %slice_bitcast_fusion = (bf16[64,96,128]{2,0,1:T(8,128)(2,1)}, bf16[64,96,128]{2,0,1:T(8,128)(2,1)}, bf16[64,96,128]{2,0,1:T(8,128)(2,1)}, bf16[64,96,128]{2,0,1...) fusion(bf16[6,96,64,128]{3,2,1,0:T(8,128)(2,1)} %param.6), kind=kLoop, calls=%fused_computation | loop fusion | bytes 18874368 | tf_op jit(solution)/shard_map/reshape | solution.py:312
  6.5 0.0 copy-start.4
  6.5 1.0 copy.16.own
  7.5 0.0 copy-start
  7.6 0.3 collective-permute-start
  7.8 0.0 copy-done.4
  7.8 0.1 copy.14
  7.9 0.0 copy-start.3
  7.9 3.8 copy.25.refs_2_.own
  11.7 0.0 copy-done
  11.7 0.0 copy-done.3
  11.7 0.0 copy-start.2
  11.7 2.2 copy.21.refs_2_.own
  13.9 0.0 copy-done.2
  13.9 0.0 copy-start.1
  13.9 2.2 copy.19.refs_2_.own
  16.1 0.0 copy-done.1
  16.1 2.2 copy.17.refs_0_.own
  18.2 0.0 copy-start.7
  18.2 0.0 copy-start.6
  18.2 0.0 copy-start.5
  18.2 2.1 copy.23.refs_2_.own
  20.4 0.0 copy-done.7
  20.4 0.7 dynamic_slice.6.refs_0_
  21.1 0.0 copy-done.6
  21.1 0.1 dynamic_slice.7
  21.1 0.0 copy-done.5
  21.1 0.7 fusion.1.tiles
  21.8 21.2 %collective-permute-done.other = bf16[64,96,128]{2,1,0:T(8,128)(2,1)} collective-permute-done((bf16[64,96,128]{2,1,0:T(8,128)(2,1)S(1)}, bf16[64,96,128]{2,1,0:T(8,128)(2,1)}, u32[]{:S(2)}, u32[]{:S(2)}) %collective-permute-start) | collective-permute-done | bytes 1572896 | tf_op jit(solution)/shard_map/ppermute | solution.py:314
  43.0 44.5 %ladder_0.1 = (f32[2,4,768,128]{3,2,1,0:T(8,128)}, s16[16,2,4,48,128]{4,3,2,1,0:T(8,128)(2,1)}, f32[2,8,128]{2,1,0:T(8,128)}, bf16[64,96,128]{2,1,0:T(8,128)(2,1)}) custom-call(s32[64,20]{1,0:T(8,128)} %fusion.1.tiles, bf16[64,96,128]{2,1,0:T(8,128)(2,1)} %copy-done, bf16[64,96,128]{2,1,0:T(8,128)(2,1)} %collective-permute-done.other, ...), custom_call_target="tpu_custom_call" | custom-call | flops 4026531840 | bytes 41943040 | tf_op jit(solution)/shard_map/ladder_0/pallas_call | solution.py:327
  87.5 63.0 %ladder_1.1 = (f32[2,4,768,128]{3,2,1,0:T(8,128)}, s16[16,2,4,48,128]{4,3,2,1,0:T(8,128)(2,1)}, f32[2,8,128]{2,1,0:T(8,128)}, s16[16,2,4,48,128]{4,3,2,1,0:T(8,1...) custom-call(s32[64,20]{1,0:T(8,128)} %fusion.1.tiles, bf16[64,96,128]{2,1,0:T(8,128)(2,1)} %copy.17.refs_0_.own, ...), custom_call_target="tpu_custom_call" | custom-call | flops 4026531840 | bytes 41943040 | tf_op jit(solution)/shard_map/ladder_1/pallas_call | solution.py:327
  150.5 63.5 %ladder_2.1 = (f32[2,4,768,128]{3,2,1,0:T(8,128)}, s16[16,2,4,48,128]{4,3,2,1,0:T(8,128)(2,1)}, f32[2,8,128]{2,1,0:T(8,128)}, s16[16,2,4,48,128]{4,3,2,1,0:T(8,1...) custom-call(s32[64,20]{1,0:T(8,128)} %fusion.1.tiles, bf16[64,96,128]{2,1,0:T(8,128)(2,1)} %copy.19.refs_2_.own, ...), custom_call_target="tpu_custom_call" | custom-call | flops 4026531840 | bytes 41943040 | tf_op jit(solution)/shard_map/ladder_2/pallas_call | solution.py:327
  214.0 63.0 %ladder_3.1 = (f32[2,4,768,128]{3,2,1,0:T(8,128)}, s16[16,2,4,48,128]{4,3,2,1,0:T(8,128)(2,1)}, f32[2,8,128]{2,1,0:T(8,128)}, s16[16,2,4,48,128]{4,3,2,1,0:T(8,1...) custom-call(s32[64,20]{1,0:T(8,128)} %fusion.1.tiles, bf16[64,96,128]{2,1,0:T(8,128)(2,1)} %copy.21.refs_2_.own, ...), custom_call_target="tpu_custom_call" | custom-call | flops 4026531840 | bytes 41943040 | tf_op jit(solution)/shard_map/ladder_3/pallas_call | solution.py:327
  277.0 63.3 %ladder_4.1 = (f32[2,4,768,128]{3,2,1,0:T(8,128)}, s16[16,2,4,48,128]{4,3,2,1,0:T(8,128)(2,1)}, f32[2,8,128]{2,1,0:T(8,128)}, s16[16,2,4,48,128]{4,3,2,1,0:T(8,1...) custom-call(s32[64,20]{1,0:T(8,128)} %fusion.1.tiles, bf16[64,96,128]{2,1,0:T(8,128)(2,1)} %copy.23.refs_2_.own, ...), custom_call_target="tpu_custom_call" | custom-call | flops 4026531840 | bytes 41943040 | tf_op jit(solution)/shard_map/ladder_4/pallas_call | solution.py:327
  340.3 49.5 %ladder_5.1 = (f32[2,4,768,128]{3,2,1,0:T(8,128)}, s16[16,2,4,48,128]{4,3,2,1,0:T(8,128)(2,1)}, f32[2,8,128]{2,1,0:T(8,128)}, s16[16,2,4,48,128]{4,3,2,1,0:T(8,128)(2,1)}, f32[16,2,8,128]{3,2,1,0:T(8,128)}) custom-call(s32[64,20]{1,0:T(8,128)} %fusion.1.tiles, bf16[64,96,128]{2,1,0:T(8,128)(2,1)} %copy.25.refs_2_.own, ...), custom_call_target="tpu_custom_call" | custom-call | flops 4026531840 | bytes 41943040 | tf_op jit(solution)/shard_map/ladder_5/pallas_call | solution.py:327
  389.8 42.8 %exchange.1 = (s16[16,2,4,48,128]{4,3,2,1,0:T(8,128)(2,1)}, f32[16,2,8,128]{3,2,1,0:T(8,128)}) custom-call(s16[16,2,4,48,128]{4,3,2,1,0:T(8,128)(2,1)} %get-tuple-element.66.refs_0_, f32[2,8,128]{2,1,0:T(8,128)} %get-tuple-element.67.refs_1_), custom_call_target="tpu_custom_call" | custom-call | tf_op jit(solution)/shard_map/exchange/pallas_call | solution.py:376
  432.7 0.7 broadcast_in_dim.6.refs_2_
  433.3 0.6 broadcast_in_dim.7.refs_3_
  434.0 30.1 %combine.1 = bf16[6,96,64,128]{3,2,1,0:T(8,128)(2,1)} custom-call(f32[6]{0:T(128)} %dynamic_slice.6.refs_0_, f32[96]{0:T(128)} %refs_1_.1, f32[64,128]{1,0:T(8,128)} %broadcast_in_dim.6.refs_2_, f32[64,128]{1,0:T(8,128)} %broadcast_in_dim.7.refs_3_, f32[2,4,16,48,128]{4,3,2,1,0:T(8,128)} %bitcast.42, f32[2,4,16,48,128]{4,3,2,1,0:T(8,128)} %bitcast.43, ...), custom_call_target="tpu_custom_call" | custom-call | tf_op jit(solution)/shard_map/combine/pallas_call | solution.py:391
Async XLA Ops:
  6.5 1.3 copy-start.4
  7.5 4.2 copy-start
  7.6 35.5 %collective-permute-start = (bf16[64,96,128]{2,1,0:T(8,128)(2,1)S(1)}, bf16[64,96,128]{2,1,0:T(8,128)(2,1)}, u32[]{:S(2)}, u32[]{:S(2)}) collective-permute-start(bf16[64,96,128]{2,1,0:T(8,128)(2,1)S(1)} %copy.16.own), channel_id=1, source_target_pairs={{0,1},{1,0},{2,3},{3,2},{4,5},{5,4},{6,7},{7,6},{8,9},{9,8},{10,11... | collective-permute-start | bytes 4718600 | tf_op jit(solution)/shard_map/ppermute | solution.py:314
  7.9 3.8 copy-start.3
  11.7 2.2 copy-start.2
  13.9 2.2 copy-start.1
  18.2 2.2 copy-start.7
  18.2 2.8 copy-start.6
  18.2 2.9 copy-start.5
